TPU v7x, 128 devices: a whole 4x4x4 slice. The times are simulated.
128 devices in a mesh: seq: 16 (over z_lo, y, core), head: 8 (over x, z_hi).
Axes of the slice: x: 4, y: 4, z: 4 (z_hi: 2, z_lo: 2; z = z_hi * 2 + z_lo), core: 2. Of those that a mesh axis runs over, the one named last changes fastest.
Arguments:
- frames: bfloat16 [8192, 2048], P('seq')
- w_query: bfloat16 [2048, 2048], P(None, 'head'), may hold values from -0.125 to 0.125
- w_key: bfloat16 [2048, 2048], P(None, 'head'), may hold values from -0.125 to 0.125
- w_value: bfloat16 [2048, 2048], P(None, 'head'), may hold values from -0.125 to 0.125
- w_out: bfloat16 [2048, 2048], P('head'), may hold values from -1 to 1
- conv_taps: float32 [31, 2048], P(None, 'head'), may hold values from -1 to 1
- conv_bias: float32 [2048], P('head'), may hold values from -1 to 1
- norm_gain: float32 [2048], replicated, may hold values from 0.5 to 1.5
- w_up: bfloat16 [2048, 8192], P(None, 'head'), may hold values from -0.125 to 0.125
- w_down: bfloat16 [8192, 2048], P('head'), may hold values from -0.0625 to 0.0625
- block_lists: int32 [64, 8], P('seq'), may hold values from 0 to 63, as said below
- block_counts: int32 [64], P('seq'), may hold values from 1 to 8, as said below
Outputs:
- layer_out: bfloat16 [8192, 2048], P('seq', 'head')
Inputs may be any that keep to these rules, and one draw needn't show every extreme that they name: `block_lists`: entry 0 of query block b's list is b itself; the 8 entries of a list are distinct block indices. `block_counts`: query block 0 has all 8 entries active.
All inputs are finite; a program needn't handle non-finite values.
Results may differ from a plain program's by a relative error of at most 0.02.
The roundings to bfloat16 on the way count: a program that leaves them out, or rounds other values in their place, can miss the bound.
Values may be sent and summed in bfloat16 or wider, within the bound.
A program may use at most 128 MiB of HBM per device.

v0:
```python
import math

import jax
import jax.numpy as jnp
from jax import lax
from jax.sharding import PartitionSpec as P

HD = 64
KERNEL = 31


def extended(cells, sides, width):
    for axis, dim in sides:
        count = lax.axis_size(axis)
        ends = count - 1
        head = lax.slice_in_dim(cells, 0, width, axis=dim)
        tail = lax.slice_in_dim(cells, cells.shape[dim] - width, cells.shape[dim], axis=dim)
        cells = jnp.concatenate(
            [
                lax.ppermute(tail, axis, [(i, (i + 1) % count) for i in range(ends)]),
                cells,
                lax.ppermute(head, axis, [((i + 1) % count, i) for i in range(ends)]),
            ],
            axis=dim,
        )
    return cells


def on_device(
    frames,
    w_query,
    w_key,
    w_value,
    w_out,
    conv_taps,
    conv_bias,
    norm_gain,
    w_up,
    w_down,
    block_lists,
    block_counts,
):
    frame_rows = frames.shape[0]
    width_dev = w_query.shape[1]
    heads_dev = width_dev // HD
    query_blocks = block_lists.shape[0]
    block_rows = frame_rows // query_blocks
    total_blocks = query_blocks * lax.axis_size("seq")
    query = jnp.dot(frames, w_query, preferred_element_type=jnp.float32).astype(jnp.bfloat16)
    keys = jnp.dot(frames, w_key, preferred_element_type=jnp.float32).astype(jnp.bfloat16)
    values = jnp.dot(frames, w_value, preferred_element_type=jnp.float32).astype(jnp.bfloat16)
    slot_live = jnp.arange(block_lists.shape[1])[None, :] < block_counts[:, None]
    hits = (block_lists[:, :, None] == jnp.arange(total_blocks)[None, None, :]) & slot_live[
        :, :, None
    ]
    table = jnp.sum(hits.astype(jnp.float32), axis=1)
    query_heads = query.reshape(frame_rows, heads_dev, HD)
    stacked = jnp.stack([keys, values])

    def allowed_of(key_start, count):
        key_block = (key_start + jnp.arange(count)) // block_rows
        onehot = (key_block[:, None] == jnp.arange(total_blocks)[None, :]).astype(jnp.float32)
        coarse = jnp.dot(table, onehot.T)
        return jnp.repeat(coarse, block_rows, axis=0) > 0.5

    def update(carry, key_part, value_part, allowed):
        run_max, run_sum, run_acc = carry
        count = key_part.shape[0]
        key_heads = key_part.reshape(count, heads_dev, HD)
        value_heads = value_part.reshape(count, heads_dev, HD)
        scores = (
            jnp.einsum("qhd,khd->hqk", query_heads, key_heads, preferred_element_type=jnp.float32)
            * 0.125
        )
        scores = jnp.where(allowed[None], scores, -1e30)
        new_max = jnp.maximum(run_max, jnp.max(scores, axis=2))
        probs = jnp.where(allowed[None], jnp.exp(scores - new_max[:, :, None]), 0.0)
        rescale = jnp.exp(run_max - new_max)
        new_sum = run_sum * rescale + jnp.sum(probs, axis=2)
        new_acc = run_acc * rescale[:, :, None] + jnp.einsum(
            "hqk,khd->hqd",
            probs.astype(jnp.bfloat16),
            value_heads,
            preferred_element_type=jnp.float32,
        )
        return (new_max, new_sum, new_acc)

    start_state = (
        jnp.full((heads_dev, frame_rows), -1e30, jnp.float32),
        jnp.zeros((heads_dev, frame_rows), jnp.float32),
        jnp.zeros((heads_dev, frame_rows, HD), jnp.float32),
    )
    carry = start_state
    piece = lax.all_gather(stacked, "seq", axis=1, tiled=True)
    count = piece.shape[1]
    step_rows = math.gcd(count, 512)
    turns = count // step_rows
    parts = piece.reshape(2, turns, step_rows, width_dev).swapaxes(0, 1)
    offsets = step_rows * jnp.arange(turns)

    def visit(inner, item):
        part, offset = item
        allowed = allowed_of(offset, step_rows)
        inner = update(inner, part[0], part[1], allowed)
        return (inner, None)

    carry, _ = lax.scan(visit, carry, (parts, offsets))
    run_max, run_sum, run_acc = carry
    attended = (
        (run_acc / run_sum[:, :, None])
        .transpose(1, 0, 2)
        .reshape(frame_rows, width_dev)
        .astype(jnp.bfloat16)
    )
    columns = w_out
    mixed = lax.psum_scatter(
        jnp.einsum("fk,kc->cf", attended, columns, preferred_element_type=jnp.float32).astype(
            jnp.bfloat16
        ),
        "head",
        scatter_dimension=0,
        tiled=True,
    ).astype(jnp.float32)
    own_start = lax.axis_index("head") * width_dev
    residual_in = lax.dynamic_slice_in_dim(frames, own_start, width_dev, 1).T.astype(jnp.float32)
    stream = (residual_in + mixed).astype(jnp.bfloat16)
    padded = extended(stream, (("seq", 1),), KERNEL // 2).astype(jnp.float32)
    conv_sum = jnp.zeros((width_dev, frame_rows), jnp.float32)
    for tap in range(KERNEL):
        conv_sum = conv_sum + conv_taps[tap][:, None] * padded[:, tap : tap + frame_rows]
    second = (stream.astype(jnp.float32) + jax.nn.silu(conv_sum + conv_bias[:, None])).astype(
        jnp.bfloat16
    )
    whole = lax.all_gather(second, "head", axis=0, tiled=True).astype(jnp.float32)
    mean = jnp.mean(whole, axis=0, keepdims=True)
    centered = whole - mean
    var = jnp.mean(centered * centered, axis=0, keepdims=True)
    normed = (centered * lax.rsqrt(var + 1e-05) * norm_gain[:, None]).astype(jnp.bfloat16)
    upper = jnp.einsum("df,dk->fk", normed, w_up, preferred_element_type=jnp.float32)
    hidden = jax.nn.silu(upper).astype(jnp.bfloat16)
    columns = w_down
    ffsum = lax.psum_scatter(
        jnp.einsum("fk,kc->cf", hidden, columns, preferred_element_type=jnp.float32).astype(
            jnp.bfloat16
        ),
        "head",
        scatter_dimension=0,
        tiled=True,
    ).astype(jnp.float32)
    return (second.astype(jnp.float32) + ffsum).astype(jnp.bfloat16).T


def solution(mesh):
    placed = (
        P("seq", None),
        P(None, "head"),
        P(None, "head"),
        P(None, "head"),
        P("head", None),
        P(None, "head"),
        P("head"),
        P(),
        P(None, "head"),
        P("head", None),
        P("seq", None),
        P("seq"),
    )
    return jax.shard_map(
        on_device, mesh=mesh, in_specs=placed, out_specs=P("seq", "head"), check_vma=False
    )
```

profile of v0, /device:TPU:0, one launch (start us, length us, event | category | flops | bytes accessed | tf_op | source)
XLA Modules:
  0.0 521.4 jit_solution(5680154871138046375)
XLA Ops:
  6.6 2.7 fusion.32
  9.3 2.6 fusion.33
  13.0 2.3 convolution_convert_fusion.2
  15.4 52.2 %all-gather.3.cloned.1.call-done = bf16[2,8192,256]{2,1,0:T(8,128)(2,1)} async-done(((bf16[2,512,256]{2,1,0:T(8,128)(2,1)}), bf16[2,8192,256]{2,1,0:T(8,128)(2,1)}) %all-gather.3.cloned.1.call-update) | async-done | bytes 8388624 | tf_op jit(solution)/shard_map/all_gather | solution.py:94
  67.5 12.3 %copy.18 = bf16[2,16,512,256]{2,3,0,1:T(8,128)(2,1)} copy(bf16[2,16,512,256]{3,2,1,0:T(8,128)(2,1)} %bitcast.121) | data formatting | bytes 16777216 | tf_op jit(solution)/shard_map/reshape | solution.py:98
  79.9 196.1 %while.17 = (s32[]{:T(128)}, f32[4,512]{1,0:T(4,128)S(1)}, f32[4,512]{1,0:T(4,128)S(1)}, f32[4,512,64]{1,2,0:T(8,128)S(1)}, s32[16]{0:T(128)S(1)}, /*index=5*/bf...) while((s32[]{:T(128)}, f32[4,512]{1,0:T(4,128)S(1)}, ...), condition=%wide.region_4.5_spmd.clone, body=%wide.region_1.4_spmd.clone.sunk | while | flops 282775552 | bytes 33960632 | solution.py:107
  81.6 1.6 broadcast_in_dim.102
  84.4 2.9 fusion.104
  87.3 3.4 fusion.105
  93.8 1.6 broadcast_in_dim.102
  96.7 2.9 fusion.104
  99.5 3.4 fusion.105
  106.1 1.6 broadcast_in_dim.102
  108.9 2.9 fusion.104
  111.8 3.4 fusion.105
  118.3 1.6 broadcast_in_dim.102
  121.2 2.9 fusion.104
  124.0 3.4 fusion.105
  130.6 1.6 broadcast_in_dim.102
  133.4 2.9 fusion.104
  136.3 3.4 fusion.105
  142.9 1.6 broadcast_in_dim.102
  145.7 2.9 fusion.104
  148.6 3.4 fusion.105
  155.1 1.6 broadcast_in_dim.102
  157.9 2.9 fusion.104
  160.8 3.4 fusion.105
  167.4 1.6 broadcast_in_dim.102
  170.2 2.9 fusion.104
  173.1 3.4 fusion.105
  179.6 1.6 broadcast_in_dim.102
  182.4 2.9 fusion.104
  185.3 3.4 fusion.105
  191.9 1.6 broadcast_in_dim.102
  194.7 2.9 fusion.104
  197.6 3.4 fusion.105
  204.1 1.6 broadcast_in_dim.102
  207.0 2.9 fusion.104
  209.8 3.4 fusion.105
  216.4 1.6 broadcast_in_dim.102
  219.2 2.9 fusion.104
  222.1 3.4 fusion.105
  228.6 1.6 broadcast_in_dim.102
  231.5 2.9 fusion.104
  234.3 3.4 fusion.105
  240.9 1.6 broadcast_in_dim.102
  243.7 2.9 fusion.104
  246.6 3.4 fusion.105
  253.1 1.6 broadcast_in_dim.102
  256.0 2.9 fusion.104
  258.8 3.4 fusion.105
  265.4 1.6 broadcast_in_dim.102
  268.2 2.9 fusion.104
  271.1 3.4 fusion.105
  276.0 2.1 fusion.23
  278.2 76.4 %reduce-scatter.3.cloned.1.call-done = bf16[256,512]{0,1:T(8,128)(2,1)} async-done(((bf16[2048,512]{0,1:T(8,128)(2,1)}), bf16[256,512]{0,1:T(8,128)(2,1)}) %reduce-scatter.3.cloned.1.call-update) | async-done | bytes 262160 | tf_op jit(solution)/shard_map/reduce_scatter | solution.py:116
  358.4 3.5 collective-permute-done.1
  361.9 2.9 add_convert_fusion.1
  365.1 59.7 %all-gather.5.cloned.1.call-done = bf16[2048,512]{0,1:T(8,128)(2,1)} async-done(((bf16[256,512]{0,1:T(8,128)(2,1)}), bf16[2048,512]{0,1:T(8,128)(2,1)}) %all-gather.5.cloned.1.call-update) | async-done | bytes 2097168 | tf_op jit(solution)/shard_map/all_gather | solution.py:134
  424.8 2.1 convert_reduce_fusion
  426.9 2.3 fusion.20
  429.2 9.6 %fusion.24 = bf16[2048,512]{0,1:T(8,128)(2,1)} fusion(bf16[1024,2048]{1,0:T(8,128)(2,1)} %param.23, bf16[2048,1024]{1,0:T(8,128)(2,1)} %param.22, bf16[2048,512]{0,1:T(8,128)(2,1)S(1)} %copy-done.2, f32[2048]{0:T(1024)S(1)} %copy-done.8, f32[512]{0:T(512)S(1)} %add_rsqrt_fusion, f32[512]{0:T(512)S(1)} %broadcast_multiply_fusion), kind=kOutput, calls=%fused_computation.42 | convolution fusion | flops 4303880192 | bytes 12595200 | tf_op jit(solution)/shard_map/fk,kc->cf/dot_general | solution.py:143
  438.9 74.3 %reduce-scatter.5.cloned.1.call-done = bf16[256,512]{0,1:T(8,128)(2,1)} async-done(((bf16[2048,512]{0,1:T(8,128)(2,1)}), bf16[256,512]{0,1:T(8,128)(2,1)}) %reduce-scatter.5.cloned.1.call-update) | async-done | bytes 262160 | tf_op jit(solution)/shard_map/reduce_scatter | solution.py:142
  513.1 1.7 fusion.68
  (236 shorter events, 74.7 us)
Async XLA Ops:
  6.5 269.5 %copy-start = (bf16[256,2048]{1,0:T(8,128)(2,1)S(1)}, bf16[256,2048]{1,0:T(8,128)(2,1)}, u32[]{:S(2)}) copy-start(bf16[256,2048]{1,0:T(8,128)(2,1)} %param.18) | copy-start | bytes 3145732
  6.5 6.3 %copy-start.9 = (s32[4]{0:T(128)S(1)}, s32[4]{0:T(128)}, u32[]{:S(2)}) copy-start(s32[4]{0:T(128)} %param.25) | copy-start | bytes 52
  6.5 6.4 %copy-start.5 = (s32[4,8]{1,0:T(4,128)S(1)}, s32[4,8]{1,0:T(4,128)}, u32[]{:S(2)}) copy-start(s32[4,8]{1,0:T(4,128)} %param.24) | copy-start | bytes 388
  6.5 6.5 %copy-start.7 = (bf16[2048,256]{1,0:T(8,128)(2,1)S(1)}, bf16[2048,256]{1,0:T(8,128)(2,1)}, u32[]{:S(2)}) copy-start(bf16[2048,256]{1,0:T(8,128)(2,1)} %param.15) | copy-start | bytes 3145732
  6.5 61.0 %all-gather.3.cloned.1.call-start = ((), (), s32[]{:S(2)}) async-start(), calls=%async_computation.2 | async-start | bytes 8912896 | tf_op jit(solution)/shard_map/all_gather | solution.py:94
  12.7 341.9 %reduce-scatter.3.cloned.1.call-start = ((), (), s32[]{:S(2)}) async-start(), calls=%async_computation.3 | async-start | bytes 2359296 | tf_op jit(solution)/shard_map/reduce_scatter | solution.py:116
  87.3 3.4 copy-start.1
  99.5 3.4 copy-start.1
  111.8 3.4 copy-start.1
  124.0 3.4 copy-start.1
  136.3 3.4 copy-start.1
  148.5 3.4 copy-start.1
  160.8 3.4 copy-start.1
  173.1 3.4 copy-start.1
  185.3 3.4 copy-start.1
  197.6 3.4 copy-start.1
  209.8 3.4 copy-start.1
  222.1 3.4 copy-start.1
  234.3 3.4 copy-start.1
  246.6 3.4 copy-start.1
  258.8 3.4 copy-start.1
  271.1 3.4 copy-start.1
  275.9 2.3 copy-start.4
  276.0 85.9 %copy-start.6 = (f32[256]{0:T(256)S(1)}, f32[256]{0:T(256)}, u32[]{:S(2)}) copy-start(f32[256]{0:T(256)} %param.20) | copy-start | bytes 3076
  278.1 146.7 %all-gather.5.cloned.1.call-start = ((), (), s32[]{:S(2)}) async-start(), calls=%async_computation.4 | async-start | bytes 2359296 | tf_op jit(solution)/shard_map/all_gather | solution.py:134
  355.7 2.6 collective-permute-start
  357.0 4.8 collective-permute-start.1
  364.8 64.4 %copy-start.8 = (f32[2048]{0:T(1024)S(1)}, f32[2048]{0:T(1024)}, u32[]{:S(2)}) copy-start(f32[2048]{0:T(1024)} %param.21) | copy-start | bytes 24580
  364.9 148.2 %reduce-scatter.5.cloned.1.call-start = ((), (), s32[]{:S(2)}) async-start(), calls=%async_computation.5 | async-start | bytes 2359296 | tf_op jit(solution)/shard_map/reduce_scatter | solution.py:142
  424.8 4.4 copy-start.2
  429.2 83.9 %copy-start.3 = (bf16[256,512]{0,1:T(8,128)(2,1)S(1)}, bf16[256,512]{0,1:T(8,128)(2,1)}, u32[]{:S(2)}) copy-start(bf16[256,512]{0,1:T(8,128)(2,1)} %add_convert_fusion.1) | copy-start | bytes 786436
Sparse Core Ops, SparseCore 0:
  12.9 54.6 all-gather.2
  278.2 76.3 reduce-scatter.2
  365.0 59.8 all-gather.4
  439.0 74.0 reduce-scatter.4
where the time goes:
time: 522 us; the launch traced here: 521 us
  waiting for transfers between devices  266 us (51%)
  matrix products  90.8 us (17%)
  other arithmetic  75.9 us (15%)
  local copies, waits for them, and re-layouts  71.2 us (14%)
  between operations  13.3 us (3%)
    reduce_scatter x1, waiting for transfers between devices, on_device(): lax.psum_scatter(jnp.einsum('fk,kc->cf', attended, columns, preferred_ele...  76.4 us
    reduce_scatter x1, waiting for transfers between devices, on_device(): lax.psum_scatter(jnp.einsum('fk,kc->cf', hidden, columns, preferred_eleme...  74.3 us
    all_gather x1, waiting for transfers between devices, on_device(): lax.all_gather(second, 'head', axis=0, tiled=True).astype(jnp.float32)  59.7 us
    reduce_sum x16, other arithmetic, update(): new_sum = run_sum * rescale + jnp.sum(probs, axis=2)  54.2 us
    all_gather x1, waiting for transfers between devices, on_device(): piece = lax.all_gather(stacked, 'seq', axis=1, tiled=True)  52.2 us
    dot_general x16, matrix products, update(): jnp.einsum('qhd,khd->hqk', query_heads, key_heads, preferred_element_type...  45.9 us
    broadcast_in_dim x16, local copies, waits for them, and re-layouts, allowed_of(): return jnp.repeat(coarse, block_rows, axis=0) > 0.5  25.6 us
    dot_general x16, matrix products, update(): jnp.einsum('hqk,khd->hqd', probs.astype(jnp.bfloat16), value_heads, prefe...  21.6 us
  transfers between devices with their start and end apart: 6, of which 5 were waited for; matrix products, arithmetic and copies ran while one was open for 0% of the time, Pallas kernels for 0%

commit v1 on v0

v1 whole, which is shorter than its diff:
```python
import jax
import jax.numpy as jnp
from jax import lax
from jax.experimental import pallas as pl
from jax.experimental.pallas import tpu as pltpu
from jax.sharding import PartitionSpec as P

HD = 64
KERNEL = 31
NEG = -1e30


def qkv_kernel(x_ref, wq_ref, wk_ref, wv_ref, q_ref, kv_ref):
    width = wq_ref.shape[1]
    x = x_ref[...]
    q_ref[...] = jnp.dot(x, wq_ref[...], preferred_element_type=jnp.float32).astype(q_ref.dtype)
    kv_ref[:, :width] = jnp.dot(x, wk_ref[...], preferred_element_type=jnp.float32).astype(
        kv_ref.dtype
    )
    kv_ref[:, width:] = jnp.dot(x, wv_ref[...], preferred_element_type=jnp.float32).astype(
        kv_ref.dtype
    )


def project(frames, w_query, w_key, w_value):
    rows, depth = frames.shape
    width = w_query.shape[1]
    tile = 128
    weight = pl.BlockSpec((depth, width), lambda i: (0, 0), pipeline_mode=pl.Buffered(1))
    return pl.pallas_call(
        qkv_kernel,
        grid=(rows // tile,),
        in_specs=[pl.BlockSpec((tile, depth), lambda i: (i, 0)), weight, weight, weight],
        out_specs=[
            pl.BlockSpec((tile, width), lambda i: (i, 0)),
            pl.BlockSpec((tile, 2 * width), lambda i: (i, 0)),
        ],
        out_shape=[
            jax.ShapeDtypeStruct((rows, width), jnp.bfloat16),
            jax.ShapeDtypeStruct((rows, 2 * width), jnp.bfloat16),
        ],
        name="qkv",
    )(frames, w_query, w_key, w_value)


def attention_kernel(lists_ref, counts_ref, q_ref, kv_hbm, out_ref, kv_buf, sems):
    query_blocks, slots = lists_ref.shape
    block = q_ref.shape[0] // query_blocks
    width = q_ref.shape[1]
    copies = []
    for b in range(query_blocks):
        for j in range(slots):
            start = pl.multiple_of(lists_ref[b, j] * block, block)
            copy = pltpu.make_async_copy(
                kv_hbm.at[pl.ds(start, block), :],
                kv_buf.at[b, pl.ds(j * block, block), :],
                sems.at[b, j],
            )
            copy.start()
            copies.append(copy)
    lane = lax.broadcasted_iota(jnp.int32, (block, 2 * HD), 1)
    low = lane < HD
    slot_col = lax.broadcasted_iota(jnp.int32, (2 * block, slots * block), 1)
    for b in range(query_blocks):
        for j in range(slots):
            copies[b * slots + j].wait()
        live = slot_col < counts_ref[b] * block
        rows = pl.ds(b * block, block)
        for pair in range(width // (2 * HD)):
            cols = pl.ds(pair * 2 * HD, 2 * HD)
            q = q_ref[rows, cols]
            zero = jnp.zeros_like(q)
            both = jnp.concatenate([jnp.where(low, q, zero), jnp.where(low, zero, q)], axis=0)
            k = kv_buf[b, :, cols]
            v = kv_buf[b, :, pl.ds(width + pair * 2 * HD, 2 * HD)]
            scores = 0.125 * lax.dot_general(
                both, k, (((1,), (1,)), ((), ())), preferred_element_type=jnp.float32
            )
            scores = jnp.where(live, scores, NEG)
            top = jnp.max(scores, axis=1, keepdims=True)
            p = jnp.exp(scores - top)
            total = jnp.sum(p, axis=1, keepdims=True)
            o = jnp.dot(p.astype(jnp.bfloat16), v, preferred_element_type=jnp.float32) / total
            out_ref[rows, cols] = jnp.where(low, o[:block], o[block:]).astype(out_ref.dtype)


def attend(lists, counts, query, kv):
    rows, width = query.shape
    query_blocks, slots = lists.shape
    block = rows // query_blocks
    return pl.pallas_call(
        attention_kernel,
        in_specs=[
            pl.BlockSpec(memory_space=pltpu.SMEM),
            pl.BlockSpec(memory_space=pltpu.SMEM),
            pl.BlockSpec(memory_space=pltpu.VMEM),
            pl.BlockSpec(memory_space=pl.ANY),
        ],
        out_specs=pl.BlockSpec(memory_space=pltpu.VMEM),
        out_shape=jax.ShapeDtypeStruct((rows, width), jnp.bfloat16),
        scratch_shapes=[
            pltpu.VMEM((query_blocks, slots * block, 2 * width), jnp.bfloat16),
            pltpu.SemaphoreType.DMA((query_blocks, slots)),
        ],
        name="attend",
    )(lists, counts, query, kv)


def extended(cells, sides, width):
    for axis, dim in sides:
        count = lax.axis_size(axis)
        ends = count - 1
        head = lax.slice_in_dim(cells, 0, width, axis=dim)
        tail = lax.slice_in_dim(cells, cells.shape[dim] - width, cells.shape[dim], axis=dim)
        cells = jnp.concatenate(
            [
                lax.ppermute(tail, axis, [(i, (i + 1) % count) for i in range(ends)]),
                cells,
                lax.ppermute(head, axis, [((i + 1) % count, i) for i in range(ends)]),
            ],
            axis=dim,
        )
    return cells


def on_device(
    frames,
    w_query,
    w_key,
    w_value,
    w_out,
    conv_taps,
    conv_bias,
    norm_gain,
    w_up,
    w_down,
    block_lists,
    block_counts,
):
    frame_rows = frames.shape[0]
    width_dev = w_query.shape[1]
    query, own_kv = project(frames, w_query, w_key, w_value)
    kv = lax.all_gather(own_kv, "seq", axis=0, tiled=True)
    attended = attend(block_lists, block_counts, query, kv)
    columns = w_out
    mixed = lax.psum_scatter(
        jnp.einsum("fk,kc->cf", attended, columns, preferred_element_type=jnp.float32).astype(
            jnp.bfloat16
        ),
        "head",
        scatter_dimension=0,
        tiled=True,
    ).astype(jnp.float32)
    own_start = lax.axis_index("head") * width_dev
    residual_in = lax.dynamic_slice_in_dim(frames, own_start, width_dev, 1).T.astype(jnp.float32)
    stream = (residual_in + mixed).astype(jnp.bfloat16)
    padded = extended(stream, (("seq", 1),), KERNEL // 2).astype(jnp.float32)
    conv_sum = jnp.zeros((width_dev, frame_rows), jnp.float32)
    for tap in range(KERNEL):
        conv_sum = conv_sum + conv_taps[tap][:, None] * padded[:, tap : tap + frame_rows]
    second = (stream.astype(jnp.float32) + jax.nn.silu(conv_sum + conv_bias[:, None])).astype(
        jnp.bfloat16
    )
    whole = lax.all_gather(second, "head", axis=0, tiled=True).astype(jnp.float32)
    mean = jnp.mean(whole, axis=0, keepdims=True)
    centered = whole - mean
    var = jnp.mean(centered * centered, axis=0, keepdims=True)
    normed = (centered * lax.rsqrt(var + 1e-05) * norm_gain[:, None]).astype(jnp.bfloat16)
    upper = jnp.einsum("df,dk->fk", normed, w_up, preferred_element_type=jnp.float32)
    hidden = jax.nn.silu(upper).astype(jnp.bfloat16)
    columns = w_down
    ffsum = lax.psum_scatter(
        jnp.einsum("fk,kc->cf", hidden, columns, preferred_element_type=jnp.float32).astype(
            jnp.bfloat16
        ),
        "head",
        scatter_dimension=0,
        tiled=True,
    ).astype(jnp.float32)
    return (second.astype(jnp.float32) + ffsum).astype(jnp.bfloat16).T


def solution(mesh):
    placed = (
        P("seq", None),
        P(None, "head"),
        P(None, "head"),
        P(None, "head"),
        P("head", None),
        P(None, "head"),
        P("head"),
        P(),
        P(None, "head"),
        P("head", None),
        P("seq", None),
        P("seq"),
    )
    return jax.shard_map(
        on_device, mesh=mesh, in_specs=placed, out_specs=P("seq", "head"), check_vma=False
    )
```

time: 522 us -> 319 us (0.61)
  matrix products: 90.8 us -> 12.6 us
  local copies, waits for them, and re-layouts: 71.2 us -> 0.07 us
  other arithmetic: 75.9 us -> 10.2 us
  Pallas kernels: 0 us -> 13.4 us
    dot_general x51 -> x0, matrix products: 79.2 us -> none  [the longest x16 45.9 us: update(): jnp.einsum('qhd,khd->hqk', query_heads, key_heads, preferred_element_type...]
    reduce_sum x17 -> x0, other arithmetic: 54.3 us -> none  [the longest x16 54.2 us: update(): new_sum = run_sum * rescale + jnp.sum(probs, axis=2)]
    broadcast_in_dim x16 -> x0, local copies, waits for them, and re-layouts: 25.6 us -> none  [allowed_of(): return jnp.repeat(coarse, block_rows, axis=0) > 0.5]
    slice x16 -> x0, local copies, waits for them, and re-layouts: 17.2 us -> none  [visit(): inner = update(inner, part[0], part[1], allowed)]
    pallas_call x0 -> x2, Pallas kernels: none -> 13.4 us  [the longest x1 7.76 us: attend(): pl.pallas_call(attention_kernel, in_specs=[pl.BlockSpec(memory_space=pltp...]
    reshape x1 -> x0, local copies, waits for them, and re-layouts: 12.3 us -> none  [on_device(): parts = piece.reshape(2, turns, step_rows, width_dev).swapaxes(0, 1)]
    dynamic_slice x16 -> x0, local copies, waits for them, and re-layouts: 10.2 us -> none  [on_device(): carry, _ = lax.scan(visit, carry, (parts, offsets))]
    select_n x16 -> x0, other arithmetic: 10 us -> none  [allowed_of(): key_block = (key_start + jnp.arange(count)) // block_rows]
where the time goes in v1:
time: 319 us
  waiting for transfers between devices  265 us (83%)
  Pallas kernels  13.4 us (4%)
  between operations  13.3 us (4%)
  matrix products  12.6 us (4%)
  other arithmetic  10.2 us (3%)
  starting transfers between devices  4.63 us (1%)
    reduce_scatter x1, waiting for transfers between devices, on_device(): lax.psum_scatter(jnp.einsum('fk,kc->cf', attended, columns, preferred_ele...  76.5 us
    reduce_scatter x1, waiting for transfers between devices, on_device(): lax.psum_scatter(jnp.einsum('fk,kc->cf', hidden, columns, preferred_eleme...  74.4 us
    all_gather x1, waiting for transfers between devices, on_device(): lax.all_gather(second, 'head', axis=0, tiled=True).astype(jnp.float32)  58.2 us
    all_gather x1, waiting for transfers between devices, on_device(): kv = lax.all_gather(own_kv, 'seq', axis=0, tiled=True)  54.7 us
    dot_general x1, matrix products, on_device(): jnp.einsum('fk,kc->cf', hidden, columns, preferred_element_type=jnp.float32)  9.57 us
    pallas_call x1, Pallas kernels, attend(): pl.pallas_call(attention_kernel, in_specs=[pl.BlockSpec(memory_space=pltp...  7.76 us
  transfers between devices with their start and end apart: 6, of which 5 were waited for; matrix products, arithmetic and copies ran while one was open for 0% of the time, Pallas kernels for 0%

profile of v1, /device:TPU:0, one launch (start us, length us, event | category | flops | bytes accessed | tf_op | source)
XLA Modules:
  0.0 318.8 jit_solution(3278901617161899951)
XLA Ops:
  6.5 0.0 copy-start
  6.5 0.0 all-gather.3.cloned.1.call-start
  6.5 5.7 %qkv.1 = (bf16[512,256]{1,0:T(8,128)(2,1)}, bf16[512,512]{1,0:T(8,128)(2,1)}) custom-call(bf16[512,2048]{1,0:T(8,128)(2,1)} %x_ref.1, bf16[2048,256]{1,0:T(8,128)(2,1)} %wq_ref.1, bf16[2048,256]{1,0:T(8,128)(2,1)} %wk_ref.1, bf16[2048,256]{1,0:T(8,128)(2,1)} %wv_ref.1), custom_call_target="tpu_custom_call" | custom-call | tf_op jit(solution)/shard_map/qkv/pallas_call | solution.py:30
  12.2 0.0 all-gather.3.cloned.1.call-update
  12.3 0.0 reduce-scatter.3.cloned.1.call-start
  12.3 54.7 %all-gather.3.cloned.1.call-done.kv_hbm = bf16[8192,512]{1,0:T(8,128)(2,1)} async-done(((bf16[512,512]{1,0:T(8,128)(2,1)}), bf16[8192,512]{1,0:T(8,128)(2,1)}) %all-gather.3.cloned.1.call-update) | async-done | bytes 8388624 | tf_op jit(solution)/shard_map/all_gather | solution.py:143
  67.0 7.8 %attend.1 = bf16[512,256]{1,0:T(8,128)(2,1)} custom-call(s32[4,8]{1,0:T(4,128)} %lists_ref.1, s32[4]{0:T(128)} %counts_ref.1, bf16[512,256]{1,0:T(8,128)(2,1)} %get-tuple-element.7.q_ref, bf16[8192,512]{1,0:T(8,128)(2,1)} %all-gather.3.cloned.1.call-done.kv_hbm), custom_call_target="tpu_custom_call" | custom-call | tf_op jit(solution)/shard_map/attend/pallas_call | solution.py:91
  74.8 0.0 copy-done
  74.8 0.0 copy-start.3
  74.8 0.0 copy-start.4
  74.8 3.0 fusion.5
  77.8 0.0 reduce-scatter.3.cloned.1.call-update
  77.9 0.0 all-gather.5.cloned.1.call-start
  77.9 0.0 copy-done.3
  78.0 76.5 %reduce-scatter.3.cloned.1.call-done = bf16[256,512]{0,1:T(8,128)(2,1)} async-done(((bf16[2048,512]{0,1:T(8,128)(2,1)}), bf16[256,512]{0,1:T(8,128)(2,1)}) %reduce-scatter.3.cloned.1.call-update) | async-done | bytes 262160 | tf_op jit(solution)/shard_map/reduce_scatter | solution.py:146
  154.4 1.1 fusion.47
  155.5 1.3 collective-permute-start.1
  156.8 3.0 collective-permute-start
  159.9 0.0 collective-permute-done.1
  159.9 0.8 collective-permute-done
  160.7 0.1 maximum_convert_fusion
  160.7 0.0 copy-done.4
  160.8 2.9 add_convert_fusion.1
  163.7 0.0 copy-start.5
  163.7 0.0 all-gather.5.cloned.1.call-update
  163.7 0.2 reduce-scatter.5.cloned.1.call-start
  163.9 58.2 %all-gather.5.cloned.1.call-done = bf16[2048,512]{0,1:T(8,128)(2,1)} async-done(((bf16[256,512]{0,1:T(8,128)(2,1)}), bf16[2048,512]{0,1:T(8,128)(2,1)}) %all-gather.5.cloned.1.call-update) | async-done | bytes 2097168 | tf_op jit(solution)/shard_map/all_gather | solution.py:164
  222.1 0.0 copy-start.1
  222.1 2.1 convert_reduce_fusion
  224.2 2.3 fusion.2
  226.5 0.0 copy-done.5
  226.5 0.0 copy-done.1
  226.5 0.0 copy-start.2
  226.6 9.6 %fusion.6 = bf16[2048,512]{0,1:T(8,128)(2,1)} fusion(bf16[1024,2048]{1,0:T(8,128)(2,1)} %param.21, bf16[2048,1024]{1,0:T(8,128)(2,1)} %param.20, bf16[2048,512]{0,1:T(8,128)(2,1)S(1)} %copy-done.1, f32[2048]{0:T(1024)S(1)} %copy-done.5, f32[512]{0:T(512)S(1)} %add_rsqrt_fusion, f32[512]{0:T(512)S(1)} %broadcast_multiply_fusion), kind=kOutput, calls=%fused_computation.10 | convolution fusion | flops 4303880192 | bytes 12595200 | tf_op jit(solution)/shard_map/fk,kc->cf/dot_general | solution.py:173
  236.1 0.0 reduce-scatter.5.cloned.1.call-update
  236.1 74.4 %reduce-scatter.5.cloned.1.call-done = bf16[256,512]{0,1:T(8,128)(2,1)} async-done(((bf16[2048,512]{0,1:T(8,128)(2,1)}), bf16[256,512]{0,1:T(8,128)(2,1)}) %reduce-scatter.5.cloned.1.call-update) | async-done | bytes 262160 | tf_op jit(solution)/shard_map/reduce_scatter | solution.py:172
  310.6 0.0 copy-done.2
  310.6 1.7 fusion.48
  (5 shorter events, 0.1 us)
Async XLA Ops:
  6.5 68.3 %copy-start = (bf16[256,2048]{1,0:T(8,128)(2,1)S(1)}, bf16[256,2048]{1,0:T(8,128)(2,1)}, u32[]{:S(2)}) copy-start(bf16[256,2048]{1,0:T(8,128)(2,1)} %param.16) | copy-start | bytes 3145732
  6.5 60.5 %all-gather.3.cloned.1.call-start = ((), (), s32[]{:S(2)}) async-start(), calls=%async_computation.2 | async-start | bytes 8912896 | tf_op jit(solution)/shard_map/all_gather | solution.py:143
  12.3 142.2 %reduce-scatter.3.cloned.1.call-start = ((), (), s32[]{:S(2)}) async-start(), calls=%async_computation.3 | async-start | bytes 2359296 | tf_op jit(solution)/shard_map/reduce_scatter | solution.py:146
  74.8 3.1 copy-start.3
  74.8 85.9 %copy-start.4 = (f32[256]{0:T(256)S(1)}, f32[256]{0:T(256)}, u32[]{:S(2)}) copy-start(f32[256]{0:T(256)} %param.18) | copy-start | bytes 3076
  77.9 144.3 %all-gather.5.cloned.1.call-start = ((), (), s32[]{:S(2)}) async-start(), calls=%async_computation.4 | async-start | bytes 2359296 | tf_op jit(solution)/shard_map/all_gather | solution.py:164
  155.5 4.4 %collective-permute-start.1 = (bf16[256,15]{0,1:T(8,128)(2,1)S(1)}, bf16[256,15]{0,1:T(8,128)(2,1)S(1)}, u32[]{:S(2)}, u32[]{:S(2)}) collective-permute-start(bf16[256,15]{0,1:T(8,128)(2,1)S(1)} %get-tuple-element.10), channel_id=1, source_target_pairs={{8,0},{16,8},{24,16},{32,24},{40,32},{48,40},{56,48},{64,56},{72,6... | collective-permute-start | bytes 23048 | tf_op jit(solution)/shard_map/ppermute | solution.py:119
  156.8 3.8 %collective-permute-start = (bf16[256,15]{0,1:T(8,128)(2,1)S(1)}, bf16[256,15]{0,1:T(8,128)(2,1)S(1)}, u32[]{:S(2)}, u32[]{:S(2)}) collective-permute-start(bf16[256,15]{0,1:T(8,128)(2,1)S(1)} %get-tuple-element.9), channel_id=1, source_target_pairs={{0,8},{8,16},{16,24},{24,32},{32,40},{40,48},{48,56},{56,64},{64,7... | collective-permute-start | bytes 23048 | tf_op jit(solution)/shard_map/ppermute | solution.py:117
  163.7 62.9 %copy-start.5 = (f32[2048]{0:T(1024)S(1)}, f32[2048]{0:T(1024)}, u32[]{:S(2)}) copy-start(f32[2048]{0:T(1024)} %param.19) | copy-start | bytes 24580
  163.7 146.9 %reduce-scatter.5.cloned.1.call-start = ((), (), s32[]{:S(2)}) async-start(), calls=%async_computation.5 | async-start | bytes 2359296 | tf_op jit(solution)/shard_map/reduce_scatter | solution.py:172
  222.1 4.4 %copy-start.1 = (bf16[2048,512]{0,1:T(8,128)(2,1)S(1)}, bf16[2048,512]{0,1:T(8,128)(2,1)}, u32[]{:S(2)}) copy-start(bf16[2048,512]{0,1:T(8,128)(2,1)} %all-gather.5.cloned.1.call-done) | copy-start | bytes 6291460
  226.5 84.0 %copy-start.2 = (bf16[256,512]{0,1:T(8,128)(2,1)S(1)}, bf16[256,512]{0,1:T(8,128)(2,1)}, u32[]{:S(2)}) copy-start(bf16[256,512]{0,1:T(8,128)(2,1)} %add_convert_fusion.1) | copy-start | bytes 786436
Sparse Core Ops, SparseCore 0:
  12.4 54.6 all-gather.2
  78.0 76.3 reduce-scatter.2
  163.8 58.2 all-gather.4
  236.3 74.2 reduce-scatter.4

commit v2 on v1

--- a/solution.py
+++ b/solution.py
@@ -1,3 +1,5 @@
+import functools
+
 import jax
 import jax.numpy as jnp
 from jax import lax
@@ -106,21 +108,357 @@
     )(lists, counts, query, kv)
 
 
-def extended(cells, sides, width):
-    for axis, dim in sides:
-        count = lax.axis_size(axis)
-        ends = count - 1
-        head = lax.slice_in_dim(cells, 0, width, axis=dim)
-        tail = lax.slice_in_dim(cells, cells.shape[dim] - width, cells.shape[dim], axis=dim)
-        cells = jnp.concatenate(
-            [
-                lax.ppermute(tail, axis, [(i, (i + 1) % count) for i in range(ends)]),
-                cells,
-                lax.ppermute(head, axis, [((i + 1) % count, i) for i in range(ends)]),
-            ],
-            axis=dim,
+MESH = pl.DeviceIdType.MESH
+PIECES = 4
+HALO = 16
+
+
+def silu(v):
+    return v / (1.0 + jnp.exp(-v))
+
+
+class Place:
+    def __init__(self, heads, seqs):
+        self.me = lax.axis_index("head")
+        ring = heads // 2
+        self.x = lax.div(self.me, 2)
+        self.z = lax.rem(self.me, 2)
+        self.x_right = lax.rem(self.x + 1, ring)
+        self.x_left = lax.rem(self.x + ring - 1, ring)
+        self.x_far = lax.rem(self.x + 2, ring)
+        self.right = {"head": self.x_right * 2 + self.z}
+        self.left = {"head": self.x_left * 2 + self.z}
+        self.partner = {"head": self.x * 2 + 1 - self.z}
+        self.s = lax.axis_index("seq")
+        self.after = {"seq": lax.rem(self.s + 1, seqs)}
+        self.before = {"seq": lax.rem(self.s + seqs - 1, seqs)}
+
+    def greet(self):
+        barrier = pltpu.get_barrier_semaphore()
+        others = (self.right, self.left, self.partner, self.after, self.before)
+        for other in others:
+            pl.semaphore_signal(barrier, inc=1, device_id=other, device_id_type=MESH)
+        pl.semaphore_wait(barrier, len(others))
+
+    def ways(self, p):
+        if p < PIECES // 2:
+            return self.right, self.left, self.x_right, self.x_left
+        return self.left, self.right, self.x_left, self.x_right
+
+
+def send(src, dst, sems, key, device):
+    copy = pltpu.make_async_remote_copy(
+        src_ref=src,
+        dst_ref=dst,
+        send_sem=sems.at[0, key],
+        recv_sem=sems.at[1, key],
+        device_id=device,
+        device_id_type=MESH,
+    )
+    copy.start()
+    return copy
+
+
+class Scatter:
+    def __init__(self, place, a, w, bufs, sems):
+        self.place, self.a, self.w = place, a, w
+        (self.relay, self.direct, self.sums, self.zbuf, self.acc) = bufs
+        self.sems = sems
+        self.rows = a.shape[0] // PIECES
+        self.width = w.shape[1] // 4
+        self.copies = {}
+
+    def part(self, p, xd):
+        cols = pl.ds(pl.multiple_of(xd * self.width, self.width), self.width)
+        return jnp.dot(
+            self.a[p * self.rows : (p + 1) * self.rows, :],
+            self.w[:, cols],
+            preferred_element_type=jnp.float32,
         )
-    return cells
+
+    def go(self, p, kind, buf, device):
+        self.copies[p, kind] = send(
+            buf.at[0, p], buf.at[1, p], self.sems, p * 4 + kind, device
+        )
+
+    def first(self, p):
+        fwd, bwd, x_fwd, x_bwd = self.place.ways(p)
+        self.relay[0, p] = self.part(p, self.place.x_far).astype(jnp.bfloat16)
+        self.go(p, 0, self.relay, fwd)
+        self.direct[0, p] = self.part(p, x_bwd).astype(jnp.bfloat16)
+        self.go(p, 1, self.direct, bwd)
+
+    def second(self, p):
+        fwd, bwd, x_fwd, x_bwd = self.place.ways(p)
+        mine = self.part(p, x_fwd)
+        self.copies[p, 0].wait_recv()
+        self.sums[0, p] = (mine + self.relay[1, p].astype(jnp.float32)).astype(jnp.bfloat16)
+        self.go(p, 2, self.sums, fwd)
+
+    def own(self, p):
+        self.acc[p] = self.part(p, self.place.x)
+
+    def third(self, p):
+        self.copies[p, 1].wait_recv()
+        self.copies[p, 2].wait_recv()
+        self.acc[p] = (
+            self.acc[p]
+            + self.direct[1, p].astype(jnp.float32)
+            + self.sums[1, p].astype(jnp.float32)
+        )
+        half = self.width // 2
+        other = pl.ds(pl.multiple_of((1 - self.place.z) * half, half), half)
+        self.zbuf[0, p] = self.acc[p, :, other].astype(jnp.bfloat16)
+        self.go(p, 3, self.zbuf, self.place.partner)
+
+    def last(self, p):
+        self.copies[p, 3].wait_recv()
+        half = self.width // 2
+        kept = pl.ds(pl.multiple_of(self.place.z * half, half), half)
+        return self.acc[p, :, kept] + self.zbuf[1, p].astype(jnp.float32)
+
+    def finish(self):
+        for copy in self.copies.values():
+            copy.wait_send()
+
+
+class Gather:
+    def __init__(self, place, whole, sems):
+        self.place, self.whole, self.sems = place, whole, sems
+        self.rows = whole.shape[0] // PIECES
+        self.width = whole.shape[1] // 8
+        self.copies = {}
+
+    def view(self, p, head, count):
+        width = self.width
+        cols = pl.ds(pl.multiple_of(head * width, width), count * width)
+        return self.whole.at[p * self.rows : (p + 1) * self.rows, cols]
+
+    def go(self, p, kind, head, count, device):
+        view = self.view(p, head, count)
+        self.copies[p, kind] = send(view, view, self.sems, p * 6 + kind, device)
+
+    def first(self, p):
+        fwd, bwd, x_fwd, x_bwd = self.place.ways(p)
+        self.go(p, 0, self.place.me, 1, self.place.partner)
+        self.go(p, 1, self.place.me, 1, fwd)
+        self.go(p, 2, self.place.me, 1, bwd)
+
+    def second(self, p):
+        fwd, bwd, x_fwd, x_bwd = self.place.ways(p)
+        self.copies[p, 0].wait_recv()
+        mate = self.place.x * 2 + 1 - self.place.z
+        self.go(p, 3, mate, 1, fwd)
+        self.go(p, 4, mate, 1, bwd)
+
+    def third(self, p):
+        fwd, bwd, x_fwd, x_bwd = self.place.ways(p)
+        self.copies[p, 1].wait_recv()
+        self.copies[p, 3].wait_recv()
+        self.go(p, 5, x_bwd * 2, 2, fwd)
+
+    def last(self, p):
+        self.copies[p, 2].wait_recv()
+        self.copies[p, 4].wait_recv()
+        self.copies[p, 5].wait_recv()
+
+    def finish(self):
+        for copy in self.copies.values():
+            copy.wait_send()
+
+
+def tail_kernel(
+    heads,
+    seqs,
+    att_ref,
+    w_out_ref,
+    frames_hbm,
+    taps_ref,
+    bias_ref,
+    gain_ref,
+    up_hbm,
+    down_hbm,
+    out_ref,
+    up,
+    down,
+    resid,
+    stream,
+    halo,
+    pad,
+    second,
+    whole,
+    hidden,
+    relay_o,
+    direct_o,
+    sums_o,
+    z_o,
+    acc_o,
+    relay_f,
+    direct_f,
+    sums_f,
+    z_f,
+    acc_f,
+    local_sems,
+    sems_o,
+    sems_h,
+    sems_g,
+    sems_f,
+):
+    place = Place(heads, seqs)
+    frame_rows, width = out_ref.shape
+    rows = frame_rows // PIECES
+    own_cols = pl.ds(pl.multiple_of(place.me * width, width), width)
+    get_resid = pltpu.make_async_copy(frames_hbm.at[:, own_cols], resid, local_sems.at[0])
+    get_up = pltpu.make_async_copy(up_hbm, up, local_sems.at[1])
+    get_down = pltpu.make_async_copy(down_hbm, down, local_sems.at[2])
+    get_resid.start()
+    get_up.start()
+    get_down.start()
+    place.greet()
+
+    outer, inner = (0, PIECES - 1), tuple(range(1, PIECES - 1))
+    mix = Scatter(place, att_ref, w_out_ref, (relay_o, direct_o, sums_o, z_o, acc_o), sems_o)
+    for p in outer:
+        mix.first(p)
+    for p in outer:
+        mix.second(p)
+    for p in inner:
+        mix.first(p)
+    for p in outer + inner:
+        mix.own(p)
+    for p in inner:
+        mix.second(p)
+    for p in outer:
+        mix.third(p)
+    get_resid.wait()
+
+    def place_stream(p):
+        at = slice(p * rows, (p + 1) * rows)
+        value = (resid[at, :].astype(jnp.float32) + mix.last(p)).astype(jnp.bfloat16)
+        stream[at, :] = value
+        pad[HALO + p * rows : HALO + (p + 1) * rows, :] = value.astype(jnp.float32)
+
+    for p in outer:
+        place_stream(p)
+    to_before = send(stream.at[0:HALO, :], halo.at[1], sems_h, 0, place.before)
+    to_after = send(
+        stream.at[frame_rows - HALO : frame_rows, :], halo.at[0], sems_h, 1, place.after
+    )
+    for p in inner:
+        mix.third(p)
+    for p in inner:
+        place_stream(p)
+    to_before.wait_recv()
+    to_after.wait_recv()
+    top = jnp.where(place.s == 0, 0.0, 1.0)
+    bottom = jnp.where(place.s == seqs - 1, 0.0, 1.0)
+    pad[0:HALO, :] = halo[0].astype(jnp.float32) * top
+    pad[HALO + frame_rows : 2 * HALO + frame_rows, :] = halo[1].astype(jnp.float32) * bottom
+
+    ring = Gather(place, whole, sems_g)
+    order = (0, PIECES - 1) + tuple(range(1, PIECES - 1))
+
+    def convolve(p):
+        shift = HALO - KERNEL // 2
+        total = jnp.zeros((rows, width), jnp.float32)
+        for tap in range(KERNEL):
+            total = total + taps_ref[tap : tap + 1, :] * pad[
+                pl.ds(p * rows + tap + shift, rows), :
+            ]
+        at = slice(p * rows, (p + 1) * rows)
+        value = pad[HALO + p * rows : HALO + (p + 1) * rows, :] + silu(total + bias_ref[...])
+        value = value.astype(jnp.bfloat16)
+        second[at, :] = value
+        whole[at, own_cols] = value
+
+    def feed(p):
+        at = slice(p * rows, (p + 1) * rows)
+        cells = whole[at, :].astype(jnp.float32)
+        mean = jnp.mean(cells, axis=1, keepdims=True)
+        centered = cells - mean
+        var = jnp.mean(centered * centered, axis=1, keepdims=True)
+        normed = (centered * lax.rsqrt(var + 1e-05) * gain_ref[...]).astype(jnp.bfloat16)
+        upper = jnp.dot(normed, up[...], preferred_element_type=jnp.float32)
+        hidden[at, :] = silu(upper).astype(jnp.bfloat16)
+
+    for p in order:
+        convolve(p)
+        ring.first(p)
+    for p in order:
+        ring.second(p)
+    for p in order[:2]:
+        ring.third(p)
+    get_up.wait()
+    get_down.wait()
+    ffn = Scatter(place, hidden, down, (relay_f, direct_f, sums_f, z_f, acc_f), sems_f)
+    for i, p in enumerate(order):
+        if i + 2 < PIECES:
+            ring.third(order[i + 2])
+        ring.last(p)
+        feed(p)
+        ffn.first(p)
+        if i >= 1:
+            ffn.second(order[i - 1])
+        ffn.own(p)
+        if i >= 2:
+            ffn.third(order[i - 2])
+    ffn.second(order[-1])
+    for p in order[-2:]:
+        ffn.third(p)
+    for p in order:
+        at = slice(p * rows, (p + 1) * rows)
+        out_ref[at, :] = (second[at, :].astype(jnp.float32) + ffn.last(p)).astype(out_ref.dtype)
+    mix.finish()
+    to_before.wait_send()
+    to_after.wait_send()
+    ring.finish()
+    ffn.finish()
+
+
+def tail(attended, w_out, frames, taps, bias, gain, w_up, w_down):
+    frame_rows, width = attended.shape
+    depth = frames.shape[1]
+    hidden = w_up.shape[1]
+    rows = frame_rows // PIECES
+    vmem = pl.BlockSpec(memory_space=pltpu.VMEM)
+    hbm = pl.BlockSpec(memory_space=pl.ANY)
+    bf16, f32 = jnp.bfloat16, jnp.float32
+    quarter = depth // 4
+    buffers = [pltpu.VMEM((2, PIECES, rows, quarter), bf16)] * 3 + [
+        pltpu.VMEM((2, PIECES, rows, width), bf16),
+        pltpu.VMEM((PIECES, rows, quarter), f32),
+    ]
+    dma = pltpu.SemaphoreType.DMA
+    return pl.pallas_call(
+        functools.partial(tail_kernel, lax.axis_size("head"), lax.axis_size("seq")),
+        in_specs=[vmem, vmem, hbm, vmem, vmem, vmem, hbm, hbm],
+        out_specs=vmem,
+        out_shape=jax.ShapeDtypeStruct((frame_rows, width), bf16),
+        scratch_shapes=[
+            pltpu.VMEM((depth, hidden), bf16),
+            pltpu.VMEM((hidden, depth), bf16),
+            pltpu.VMEM((frame_rows, width), bf16),
+            pltpu.VMEM((frame_rows, width), bf16),
+            pltpu.VMEM((2, HALO, width), bf16),
+            pltpu.VMEM((frame_rows + 2 * HALO, width), f32),
+            pltpu.VMEM((frame_rows, width), bf16),
+            pltpu.VMEM((frame_rows, depth), bf16),
+            pltpu.VMEM((frame_rows, hidden), bf16),
+        ]
+        + buffers
+        + buffers
+        + [
+            dma((3,)),
+            dma((2, PIECES * 4)),
+            dma((2, 2)),
+            dma((2, PIECES * 6)),
+            dma((2, PIECES * 4)),
+        ],
+        compiler_params=pltpu.CompilerParams(
+            collective_id=0, has_side_effects=True, vmem_limit_bytes=60 * 1024 * 1024
+        ),
+        name="tail",
+    )(attended, w_out, frames, taps, bias[None, :], gain[None, :], w_up, w_down)
 
 
 def on_device(
@@ -137,47 +475,10 @@
     block_lists,
     block_counts,
 ):
-    frame_rows = frames.shape[0]
-    width_dev = w_query.shape[1]
     query, own_kv = project(frames, w_query, w_key, w_value)
     kv = lax.all_gather(own_kv, "seq", axis=0, tiled=True)
     attended = attend(block_lists, block_counts, query, kv)
-    columns = w_out
-    mixed = lax.psum_scatter(
-        jnp.einsum("fk,kc->cf", attended, columns, preferred_element_type=jnp.float32).astype(
-            jnp.bfloat16
-        ),
-        "head",
-        scatter_dimension=0,
-        tiled=True,
-    ).astype(jnp.float32)
-    own_start = lax.axis_index("head") * width_dev
-    residual_in = lax.dynamic_slice_in_dim(frames, own_start, width_dev, 1).T.astype(jnp.float32)
-    stream = (residual_in + mixed).astype(jnp.bfloat16)
-    padded = extended(stream, (("seq", 1),), KERNEL // 2).astype(jnp.float32)
-    conv_sum = jnp.zeros((width_dev, frame_rows), jnp.float32)
-    for tap in range(KERNEL):
-        conv_sum = conv_sum + conv_taps[tap][:, None] * padded[:, tap : tap + frame_rows]
-    second = (stream.astype(jnp.float32) + jax.nn.silu(conv_sum + conv_bias[:, None])).astype(
-        jnp.bfloat16
-    )
-    whole = lax.all_gather(second, "head", axis=0, tiled=True).astype(jnp.float32)
-    mean = jnp.mean(whole, axis=0, keepdims=True)
-    centered = whole - mean
-    var = jnp.mean(centered * centered, axis=0, keepdims=True)
-    normed = (centered * lax.rsqrt(var + 1e-05) * norm_gain[:, None]).astype(jnp.bfloat16)
-    upper = jnp.einsum("df,dk->fk", normed, w_up, preferred_element_type=jnp.float32)
-    hidden = jax.nn.silu(upper).astype(jnp.bfloat16)
-    columns = w_down
-    ffsum = lax.psum_scatter(
-        jnp.einsum("fk,kc->cf", hidden, columns, preferred_element_type=jnp.float32).astype(
-            jnp.bfloat16
-        ),
-        "head",
-        scatter_dimension=0,
-        tiled=True,
-    ).astype(jnp.float32)
-    return (second.astype(jnp.float32) + ffsum).astype(jnp.bfloat16).T
+    return tail(attended, w_out, frames, conv_taps, conv_bias, norm_gain, w_up, w_down)
 
 
 def solution(mesh):

time: 319 us -> 166 us (0.52)
  waiting for transfers between devices: 265 us -> 54.8 us
  Pallas kernels: 13.4 us -> 95.7 us
  matrix products: 12.6 us -> 0 us
  other arithmetic: 10.2 us -> 0 us
  starting transfers between devices: 4.63 us -> 0.01 us
    reduce_scatter x2 -> x0, waiting for transfers between devices: 151 us -> none  [the longest x1 76.5 us: on_device(): lax.psum_scatter(jnp.einsum('fk,kc->cf', attended, columns, preferred_ele...]
    pallas_call x0 -> x1, Pallas kernels: none -> 82.4 us  [tail(): pl.pallas_call(functools.partial(tail_kernel, lax.axis_size('head'), lax....]
    all_gather x1 -> x0, waiting for transfers between devices: 58.2 us -> none  [on_device(): lax.all_gather(second, 'head', axis=0, tiled=True).astype(jnp.float32)]
    dot_general x2 -> x0, matrix products: 12.6 us -> none  [the longest x1 9.57 us: on_device(): jnp.einsum('fk,kc->cf', hidden, columns, preferred_element_type=jnp.float32)]
    reduce_sum x2 -> x0, other arithmetic: 4.36 us -> none  [the longest x1 2.27 us: on_device(): var = jnp.mean(centered * centered, axis=0, keepdims=True)]
    ppermute x2 -> x0, starting transfers between devices: 4.32 us -> none  [the longest x1 3.03 us: extended(): lax.ppermute(tail, axis, [(i, (i + 1) % count) for i in range(ends)])]
    convert_element_type x3 -> x0, other arithmetic: 4.07 us -> none  [the longest x1 2.92 us: on_device(): (stream.astype(jnp.float32) + jax.nn.silu(conv_sum + conv_bias[:, None]))...]
  transfers between devices with their start and end apart: 6 -> 1, of which waited for: 5 -> 1; matrix products, arithmetic and copies ran while one was open for 0% -> 0% of each run, Pallas kernels for 0% -> 0%
where the time goes in v2:
time: 166 us
  Pallas kernels  95.7 us (58%)
  waiting for transfers between devices  54.8 us (33%)
  between operations  13.4 us (8%)
  local copies, waits for them, and re-layouts  1.67 us (1%)
    pallas_call x1, Pallas kernels, tail(): pl.pallas_call(functools.partial(tail_kernel, lax.axis_size('head'), lax....  82.4 us
    all_gather x1, waiting for transfers between devices, on_device(): kv = lax.all_gather(own_kv, 'seq', axis=0, tiled=True)  54.8 us
    pallas_call x1, Pallas kernels, attend(): pl.pallas_call(attention_kernel, in_specs=[pl.BlockSpec(memory_space=pltp...  7.75 us
    pallas_call x1, Pallas kernels, project(): pl.pallas_call(qkv_kernel, grid=(rows // tile,), in_specs=[pl.BlockSpec((...  5.6 us
  transfers between devices with their start and end apart: 1, of which 1 were waited for; matrix products, arithmetic and copies ran while one was open for 0% of the time, Pallas kernels for 0%

profile of v2, /device:TPU:0, one launch (start us, length us, event | category | flops | bytes accessed | tf_op | source)
XLA Modules:
  0.0 165.6 jit_solution(634139580319089454)
XLA Ops:
  6.5 0.0 all-gather.2.cloned.1.call-start
  6.5 5.6 %qkv.1 = (bf16[512,256]{1,0:T(8,128)(2,1)}, bf16[512,512]{1,0:T(8,128)(2,1)}) custom-call(bf16[512,2048]{1,0:T(8,128)(2,1)} %frames_hbm.1, bf16[2048,256]{1,0:T(8,128)(2,1)} %wq_ref.1, bf16[2048,256]{1,0:T(8,128)(2,1)} %wk_ref.1, bf16[2048,256]{1,0:T(8,128)(2,1)} %wv_ref.1), custom_call_target="tpu_custom_call" | custom-call | tf_op jit(solution)/shard_map/qkv/pallas_call | solution.py:32
  12.1 0.0 all-gather.2.cloned.1.call-update
  12.2 54.8 %all-gather.2.cloned.1.call-done.kv_hbm = bf16[8192,512]{1,0:T(8,128)(2,1)} async-done(((bf16[512,512]{1,0:T(8,128)(2,1)}), bf16[8192,512]{1,0:T(8,128)(2,1)}) %all-gather.2.cloned.1.call-update) | async-done | bytes 8388624 | tf_op jit(solution)/shard_map/all_gather | solution.py:479
  66.9 7.8 %attend.1.att_ref = bf16[512,256]{1,0:T(8,128)(2,1)} custom-call(s32[4,8]{1,0:T(4,128)} %lists_ref.1, s32[4]{0:T(128)} %counts_ref.1, bf16[512,256]{1,0:T(8,128)(2,1)} %get-tuple-element.7.q_ref, bf16[8192,512]{1,0:T(8,128)(2,1)} %all-gather.2.cloned.1.call-done.kv_hbm), custom_call_target="tpu_custom_call" | custom-call | tf_op jit(solution)/shard_map/attend/pallas_call | solution.py:93
  74.7 82.4 %tail.1 = bf16[512,256]{1,0:T(8,128)(2,1)} custom-call(bf16[512,256]{1,0:T(8,128)(2,1)} %attend.1.att_ref, bf16[256,2048]{1,0:T(8,128)(2,1)} %w_out_ref.1, bf16[512,2048]{1,0:T(8,128)(2,1)} %frames_hbm.1, f32[31,256]{1,0:T(8,128)} %taps_ref.1, f32[1,256]{1,0:T(1,128)} %bitcast.3, f32[1,2048]{1,0:T(1,128)} %bitcast.2, bf16[2048,1024]{1,0:T(8,128)(2,1)} %up_hbm.1, ...), custom_call_target="tpu_custom_call" | custom-call | tf_op jit(solution)/shard_map/tail/pallas_call | solution.py:432
  157.1 1.7 %copy.14 = bf16[512,256]{1,0:T(8,128)(2,1)} copy(bf16[512,256]{1,0:T(8,128)(2,1)} %tail.1) | data formatting | bytes 524288
Async XLA Ops:
  6.5 60.4 %all-gather.2.cloned.1.call-start = ((), (), s32[]{:S(2)}) async-start(), calls=%async_computation | async-start | bytes 8912896 | tf_op jit(solution)/shard_map/all_gather | solution.py:479
Sparse Core Ops, SparseCore 0:
  12.3 54.6 all-gather.1

commit v3 on v2

--- a/solution.py
+++ b/solution.py
@@ -12,105 +12,13 @@
 NEG = -1e30
 
 
-def qkv_kernel(x_ref, wq_ref, wk_ref, wv_ref, q_ref, kv_ref):
-    width = wq_ref.shape[1]
-    x = x_ref[...]
-    q_ref[...] = jnp.dot(x, wq_ref[...], preferred_element_type=jnp.float32).astype(q_ref.dtype)
-    kv_ref[:, :width] = jnp.dot(x, wk_ref[...], preferred_element_type=jnp.float32).astype(
-        kv_ref.dtype
-    )
-    kv_ref[:, width:] = jnp.dot(x, wv_ref[...], preferred_element_type=jnp.float32).astype(
-        kv_ref.dtype
-    )
-
-
-def project(frames, w_query, w_key, w_value):
-    rows, depth = frames.shape
-    width = w_query.shape[1]
-    tile = 128
-    weight = pl.BlockSpec((depth, width), lambda i: (0, 0), pipeline_mode=pl.Buffered(1))
-    return pl.pallas_call(
-        qkv_kernel,
-        grid=(rows // tile,),
-        in_specs=[pl.BlockSpec((tile, depth), lambda i: (i, 0)), weight, weight, weight],
-        out_specs=[
-            pl.BlockSpec((tile, width), lambda i: (i, 0)),
-            pl.BlockSpec((tile, 2 * width), lambda i: (i, 0)),
-        ],
-        out_shape=[
-            jax.ShapeDtypeStruct((rows, width), jnp.bfloat16),
-            jax.ShapeDtypeStruct((rows, 2 * width), jnp.bfloat16),
-        ],
-        name="qkv",
-    )(frames, w_query, w_key, w_value)
-
-
-def attention_kernel(lists_ref, counts_ref, q_ref, kv_hbm, out_ref, kv_buf, sems):
-    query_blocks, slots = lists_ref.shape
-    block = q_ref.shape[0] // query_blocks
-    width = q_ref.shape[1]
-    copies = []
-    for b in range(query_blocks):
-        for j in range(slots):
-            start = pl.multiple_of(lists_ref[b, j] * block, block)
-            copy = pltpu.make_async_copy(
-                kv_hbm.at[pl.ds(start, block), :],
-                kv_buf.at[b, pl.ds(j * block, block), :],
-                sems.at[b, j],
-            )
-            copy.start()
-            copies.append(copy)
-    lane = lax.broadcasted_iota(jnp.int32, (block, 2 * HD), 1)
-    low = lane < HD
-    slot_col = lax.broadcasted_iota(jnp.int32, (2 * block, slots * block), 1)
-    for b in range(query_blocks):
-        for j in range(slots):
-            copies[b * slots + j].wait()
-        live = slot_col < counts_ref[b] * block
-        rows = pl.ds(b * block, block)
-        for pair in range(width // (2 * HD)):
-            cols = pl.ds(pair * 2 * HD, 2 * HD)
-            q = q_ref[rows, cols]
-            zero = jnp.zeros_like(q)
-            both = jnp.concatenate([jnp.where(low, q, zero), jnp.where(low, zero, q)], axis=0)
-            k = kv_buf[b, :, cols]
-            v = kv_buf[b, :, pl.ds(width + pair * 2 * HD, 2 * HD)]
-            scores = 0.125 * lax.dot_general(
-                both, k, (((1,), (1,)), ((), ())), preferred_element_type=jnp.float32
-            )
-            scores = jnp.where(live, scores, NEG)
-            top = jnp.max(scores, axis=1, keepdims=True)
-            p = jnp.exp(scores - top)
-            total = jnp.sum(p, axis=1, keepdims=True)
-            o = jnp.dot(p.astype(jnp.bfloat16), v, preferred_element_type=jnp.float32) / total
-            out_ref[rows, cols] = jnp.where(low, o[:block], o[block:]).astype(out_ref.dtype)
-
-
-def attend(lists, counts, query, kv):
-    rows, width = query.shape
-    query_blocks, slots = lists.shape
-    block = rows // query_blocks
-    return pl.pallas_call(
-        attention_kernel,
-        in_specs=[
-            pl.BlockSpec(memory_space=pltpu.SMEM),
-            pl.BlockSpec(memory_space=pltpu.SMEM),
-            pl.BlockSpec(memory_space=pltpu.VMEM),
-            pl.BlockSpec(memory_space=pl.ANY),
-        ],
-        out_specs=pl.BlockSpec(memory_space=pltpu.VMEM),
-        out_shape=jax.ShapeDtypeStruct((rows, width), jnp.bfloat16),
-        scratch_shapes=[
-            pltpu.VMEM((query_blocks, slots * block, 2 * width), jnp.bfloat16),
-            pltpu.SemaphoreType.DMA((query_blocks, slots)),
-        ],
-        name="attend",
-    )(lists, counts, query, kv)
-
-
 MESH = pl.DeviceIdType.MESH
 PIECES = 4
 HALO = 16
+YS = 4
+BLOCK = 128
+SLOTS = 8
+COUNT_ROW = 4
 
 
 def silu(v):
@@ -130,15 +38,25 @@
         self.left = {"head": self.x_left * 2 + self.z}
         self.partner = {"head": self.x * 2 + 1 - self.z}
         self.s = lax.axis_index("seq")
+        self.core = lax.rem(self.s, 2)
+        self.y = lax.rem(lax.div(self.s, 2), YS)
+        self.zl = lax.div(self.s, 2 * YS)
         self.after = {"seq": lax.rem(self.s + 1, seqs)}
         self.before = {"seq": lax.rem(self.s + seqs - 1, seqs)}
 
     def greet(self):
         barrier = pltpu.get_barrier_semaphore()
-        others = (self.right, self.left, self.partner, self.after, self.before)
+        others = [self.right, self.left, self.partner, self.after, self.before]
+        others += [self.far(d) for d in range(1, YS)]
         for other in others:
             pl.semaphore_signal(barrier, inc=1, device_id=other, device_id_type=MESH)
         pl.semaphore_wait(barrier, len(others))
+
+    def seq_of(self, z_at, y_at, core_at):
+        return (z_at * YS + y_at) * 2 + core_at
+
+    def far(self, d):
+        return {"seq": self.seq_of(self.zl, lax.rem(self.y + d, YS), self.core)}
 
     def ways(self, p):
         if p < PIECES // 2:
@@ -157,6 +75,215 @@
     )
     copy.start()
     return copy
+
+
+def swap(value):
+    return pltpu.roll(value, HD, 1)
+
+
+def front_kernel(
+    frames_hbm,
+    wq_hbm,
+    wk_hbm,
+    wv_hbm,
+    lists_ref,
+    counts_ref,
+    kv_all,
+    q_all,
+    tables,
+    table,
+    x,
+    wq,
+    wk,
+    wv,
+    kv_out,
+    q_out,
+    local_sems,
+    sems,
+):
+    frame_rows = x.shape[0]
+    half = frame_rows // 2
+    f32, bf16 = jnp.float32, jnp.bfloat16
+    loads = []
+    for i, (src, dst) in enumerate(
+        ((frames_hbm, x), (wk_hbm, wk), (wv_hbm, wv), (wq_hbm, wq))
+    ):
+        load = pltpu.make_async_copy(src, dst, local_sems.at[i])
+        load.start()
+        loads.append(load)
+
+    table[...] = jnp.zeros_like(table)
+    table[: lists_ref.shape[0], : lists_ref.shape[1]] = lists_ref[...]
+    table[COUNT_ROW : COUNT_ROW + 1, : counts_ref.shape[1]] = counts_ref[...]
+
+    s = lax.axis_index("seq")
+    core = lax.rem(s, 2)
+    y = lax.rem(lax.div(s, 2), YS)
+    zl = lax.div(s, 2 * YS)
+
+    def seq_of(z_at, y_at, core_at):
+        return (z_at * YS + y_at) * 2 + core_at
+
+    def far(d):
+        return {"seq": seq_of(zl, lax.rem(y + d, YS), core)}
+
+    mate = {"seq": seq_of(zl, y, 1 - core)}
+    across = {"seq": seq_of(1 - zl, y, core)}
+    barrier = pltpu.get_barrier_semaphore()
+    others = [far(d) for d in range(1, YS)] + [mate, across]
+    for other in others:
+        pl.semaphore_signal(barrier, inc=1, device_id=other, device_id_type=MESH)
+
+    low = lax.broadcasted_iota(jnp.int32, (half, 2 * HD), 1) < HD
+    for load in loads[:3]:
+        load.wait()
+    for part in range(2):
+        rows = slice(part * half, (part + 1) * half)
+        k = jnp.dot(x[rows, :], wk[...], preferred_element_type=f32)
+        v = jnp.dot(x[rows, :], wv[...], preferred_element_type=f32)
+        for pair in range(YS // 2):
+            cols = slice(pair * 2 * HD, (pair + 1) * 2 * HD)
+            kp, vp = k[:, cols], v[:, cols]
+            kv_out[2 * pair, rows, :] = jnp.where(low, kp, swap(vp)).astype(bf16)
+            kv_out[2 * pair + 1, rows, :] = jnp.where(low, swap(kp), vp).astype(bf16)
+    pl.semaphore_wait(barrier, len(others))
+
+    def rows_of(z_at, y_at, core_at):
+        start = seq_of(z_at, y_at, core_at) * frame_rows
+        return kv_all.at[pl.ds(pl.multiple_of(start, frame_rows), frame_rows), :]
+
+    sent = {}
+    here = rows_of(zl, y, core)
+    for d in (2, 1, 3):
+        to = lax.rem(y + d, YS)
+        sent["kv", d] = send(kv_out.at[to], here, sems, d, far(d))
+        sent["table", d] = send(table, tables.at[y], sems, 4 + d, far(d))
+    sent["across", 0] = send(kv_out.at[y], here, sems, 8, across)
+    sent["mate", 0] = send(kv_out.at[y], here, sems, 12, mate)
+    keep = [
+        pltpu.make_async_copy(kv_out.at[y], here, local_sems.at[4]),
+        pltpu.make_async_copy(table, tables.at[y], local_sems.at[5]),
+    ]
+    for copy in keep:
+        copy.start()
+
+    loads[3].wait()
+    q = 0.125 * jnp.dot(x[...], wq[...], preferred_element_type=f32)
+    for pair in range(YS // 2):
+        cols = slice(pair * 2 * HD, (pair + 1) * 2 * HD)
+        top, bottom = q[:half, cols], q[half:, cols]
+        q_out[2 * pair] = jnp.where(low, top, swap(bottom)).astype(bf16)
+        q_out[2 * pair + 1] = jnp.where(low, swap(top), bottom).astype(bf16)
+    for d in (2, 1, 3):
+        to = lax.rem(y + d, YS)
+        sent["q", d] = send(q_out.at[to], q_all.at[y], sems, 20 + d, far(d))
+    keep.append(pltpu.make_async_copy(q_out.at[y], q_all.at[y], local_sems.at[6]))
+    keep[-1].start()
+
+    for d in (1, 3, 2):
+        sent["kv", d].wait_recv()
+        piece = rows_of(zl, lax.rem(y + YS - d, YS), core)
+        sent["across", d] = send(piece, piece, sems, 8 + d, across)
+        sent["mate", d] = send(piece, piece, sems, 12 + d, mate)
+    for d in (0, 1, 3, 2):
+        sent["across", d].wait_recv()
+        piece = rows_of(1 - zl, lax.rem(y + YS - d, YS), core)
+        sent["over", d] = send(piece, piece, sems, 16 + d, mate)
+    for d in range(1, YS):
+        sent["table", d].wait_recv()
+    for d in range(1, YS):
+        sent["q", d].wait_recv()
+    for d in range(YS):
+        sent["mate", d].wait_recv()
+    for d in range(YS):
+        sent["over", d].wait_recv()
+    for copy in keep:
+        copy.wait()
+    for copy in sent.values():
+        copy.wait_send()
+
+
+def attention_kernel(tables_ref, q_ref, kv_ref, out_ref):
+    f32, bf16 = jnp.float32, jnp.bfloat16
+    sources, half, lanes = q_ref.shape
+    block, slots = BLOCK, SLOTS
+    per_half = half // block
+    low = lax.broadcasted_iota(jnp.int32, (block, lanes), 1) < HD
+    slot_col = lax.broadcasted_iota(jnp.int32, (block, slots * block), 1)
+
+    def attend(source, b):
+        packed = q_ref[source, (b % per_half) * block : (b % per_half + 1) * block, :]
+        packed = packed.astype(f32)
+        if b >= per_half:
+            packed = swap(packed)
+        query = jnp.where(low, packed, 0.0).astype(bf16)
+        cells = []
+        for j in range(slots):
+            start = pl.multiple_of(tables_ref[source, b, j] * block, block)
+            cells.append(kv_ref[pl.ds(start, block), :])
+        kv = jnp.concatenate(cells, axis=0)
+        scores = lax.dot_general(query, kv, (((1,), (1,)), ((), ())), preferred_element_type=f32)
+        live = slot_col < tables_ref[source, COUNT_ROW, b] * block
+        scores = jnp.where(live, scores, NEG)
+        top = jnp.max(scores, axis=1, keepdims=True)
+        p = jnp.exp(scores - top)
+        total = jnp.sum(p, axis=1, keepdims=True)
+        return jnp.dot(p.astype(bf16), kv, preferred_element_type=f32) / total
+
+    for source in range(sources):
+        for b in range(per_half):
+            early, late = attend(source, b), attend(source, b + per_half)
+            rows = slice(b * block, (b + 1) * block)
+            out_ref[source, rows, :] = jnp.where(low, swap(early), late).astype(bf16)
+
+
+def attend_listed(tables, q_all, kv_all):
+    vmem = pl.BlockSpec(memory_space=pltpu.VMEM)
+    return pl.pallas_call(
+        attention_kernel,
+        in_specs=[pl.BlockSpec(memory_space=pltpu.SMEM), vmem, vmem],
+        out_specs=vmem,
+        out_shape=jax.ShapeDtypeStruct(q_all.shape, jnp.bfloat16),
+        compiler_params=pltpu.CompilerParams(vmem_limit_bytes=32 * 1024 * 1024),
+        name="attend",
+    )(tables, q_all, kv_all)
+
+
+def front(frames, w_query, w_key, w_value, lists, counts):
+    frame_rows, depth = frames.shape
+    width = w_query.shape[1]
+    seqs = lax.axis_size("seq")
+    bf16 = jnp.bfloat16
+    hbm = pl.BlockSpec(memory_space=pltpu.HBM)
+    free = pl.BlockSpec(memory_space=pl.ANY)
+    vmem = pl.BlockSpec(memory_space=pltpu.VMEM)
+    dma = pltpu.SemaphoreType.DMA
+    lanes = 2 * HD
+    return pl.pallas_call(
+        front_kernel,
+        in_specs=[hbm, hbm, hbm, hbm, vmem, vmem],
+        out_specs=[free, free, free],
+        out_shape=[
+            jax.ShapeDtypeStruct((seqs * frame_rows, lanes), bf16),
+            jax.ShapeDtypeStruct((YS, frame_rows // 2, lanes), bf16),
+            jax.ShapeDtypeStruct((YS, 8, 128), jnp.int32),
+        ],
+        scratch_shapes=[
+            pltpu.VMEM((8, 128), jnp.int32),
+            pltpu.VMEM((frame_rows, depth), bf16),
+            pltpu.VMEM((depth, width), bf16),
+            pltpu.VMEM((depth, width), bf16),
+            pltpu.VMEM((depth, width), bf16),
+            pltpu.VMEM((YS, frame_rows, lanes), bf16),
+            pltpu.VMEM((YS, frame_rows // 2, lanes), bf16),
+            dma((7,)),
+            dma((2, 24)),
+        ],
+        compiler_params=pltpu.CompilerParams(
+            collective_id=1, has_side_effects=True, vmem_limit_bytes=48 * 1024 * 1024
+        ),
+        name="front",
+    )(frames, w_query, w_key, w_value, lists, counts[None, :])
 
 
 class Scatter:
@@ -271,7 +398,7 @@
     heads,
     seqs,
     att_ref,
-    w_out_ref,
+    w_out_hbm,
     frames_hbm,
     taps_ref,
     bias_ref,
@@ -279,6 +406,7 @@
     up_hbm,
     down_hbm,
     out_ref,
+    w_out,
     up,
     down,
     resid,
@@ -298,7 +426,10 @@
     sums_f,
     z_f,
     acc_f,
+    ret_in,
+    attended,
     local_sems,
+    sems_r,
     sems_o,
     sems_h,
     sems_g,
@@ -311,13 +442,35 @@
     get_resid = pltpu.make_async_copy(frames_hbm.at[:, own_cols], resid, local_sems.at[0])
     get_up = pltpu.make_async_copy(up_hbm, up, local_sems.at[1])
     get_down = pltpu.make_async_copy(down_hbm, down, local_sems.at[2])
+    get_out = pltpu.make_async_copy(w_out_hbm, w_out, local_sems.at[4])
+    get_out.start()
     get_resid.start()
     get_up.start()
     get_down.start()
     place.greet()
 
+    back = [
+        send(att_ref.at[lax.rem(place.y + d, YS)], ret_in.at[place.y], sems_r, d, place.far(d))
+        for d in (2, 1, 3)
+    ]
+    own_back = pltpu.make_async_copy(
+        att_ref.at[place.y], ret_in.at[place.y], local_sems.at[3]
+    )
+    own_back.start()
+    half = frame_rows // 2
+    low = lax.broadcasted_iota(jnp.int32, (half, 2 * HD), 1) < HD
+    own_back.wait()
+    for copy in back:
+        copy.wait_recv()
+    for pair in range(YS // 2):
+        cols = slice(pair * 2 * HD, (pair + 1) * 2 * HD)
+        one, two = ret_in[2 * pair].astype(jnp.float32), ret_in[2 * pair + 1].astype(jnp.float32)
+        attended[:half, cols] = jnp.where(low, one, swap(two)).astype(jnp.bfloat16)
+        attended[half:, cols] = jnp.where(low, swap(one), two).astype(jnp.bfloat16)
+
     outer, inner = (0, PIECES - 1), tuple(range(1, PIECES - 1))
-    mix = Scatter(place, att_ref, w_out_ref, (relay_o, direct_o, sums_o, z_o, acc_o), sems_o)
+    get_out.wait()
+    mix = Scatter(place, attended, w_out, (relay_o, direct_o, sums_o, z_o, acc_o), sems_o)
     for p in outer:
         mix.first(p)
     for p in outer:
@@ -408,6 +561,8 @@
     for p in order:
         at = slice(p * rows, (p + 1) * rows)
         out_ref[at, :] = (second[at, :].astype(jnp.float32) + ffn.last(p)).astype(out_ref.dtype)
+    for copy in back:
+        copy.wait_send()
     mix.finish()
     to_before.wait_send()
     to_after.wait_send()
@@ -416,12 +571,13 @@
 
 
 def tail(attended, w_out, frames, taps, bias, gain, w_up, w_down):
-    frame_rows, width = attended.shape
-    depth = frames.shape[1]
+    width = w_out.shape[0]
+    frame_rows, depth = frames.shape
     hidden = w_up.shape[1]
     rows = frame_rows // PIECES
     vmem = pl.BlockSpec(memory_space=pltpu.VMEM)
-    hbm = pl.BlockSpec(memory_space=pl.ANY)
+    hbm = pl.BlockSpec(memory_space=pltpu.HBM)
+    free = pl.BlockSpec(memory_space=pl.ANY)
     bf16, f32 = jnp.bfloat16, jnp.float32
     quarter = depth // 4
     buffers = [pltpu.VMEM((2, PIECES, rows, quarter), bf16)] * 3 + [
@@ -431,10 +587,11 @@
     dma = pltpu.SemaphoreType.DMA
     return pl.pallas_call(
         functools.partial(tail_kernel, lax.axis_size("head"), lax.axis_size("seq")),
-        in_specs=[vmem, vmem, hbm, vmem, vmem, vmem, hbm, hbm],
+        in_specs=[free, hbm, hbm, vmem, vmem, vmem, hbm, hbm],
         out_specs=vmem,
         out_shape=jax.ShapeDtypeStruct((frame_rows, width), bf16),
         scratch_shapes=[
+            pltpu.VMEM((width, depth), bf16),
             pltpu.VMEM((depth, hidden), bf16),
             pltpu.VMEM((hidden, depth), bf16),
             pltpu.VMEM((frame_rows, width), bf16),
@@ -448,14 +605,17 @@
         + buffers
         + buffers
         + [
-            dma((3,)),
+            pltpu.VMEM((YS, frame_rows // 2, 2 * HD), bf16),
+            pltpu.VMEM((frame_rows, width), bf16),
+            dma((5,)),
+            dma((2, YS)),
             dma((2, PIECES * 4)),
             dma((2, 2)),
             dma((2, PIECES * 6)),
             dma((2, PIECES * 4)),
         ],
         compiler_params=pltpu.CompilerParams(
-            collective_id=0, has_side_effects=True, vmem_limit_bytes=60 * 1024 * 1024
+            collective_id=0, has_side_effects=True, vmem_limit_bytes=44 * 1024 * 1024
         ),
         name="tail",
     )(attended, w_out, frames, taps, bias[None, :], gain[None, :], w_up, w_down)
@@ -475,9 +635,10 @@
     block_lists,
     block_counts,
 ):
-    query, own_kv = project(frames, w_query, w_key, w_value)
-    kv = lax.all_gather(own_kv, "seq", axis=0, tiled=True)
-    attended = attend(block_lists, block_counts, query, kv)
+    kv_all, q_all, tables = front(
+        frames, w_query, w_key, w_value, block_lists, block_counts
+    )
+    attended = attend_listed(tables, q_all, kv_all)
     return tail(attended, w_out, frames, conv_taps, conv_bias, norm_gain, w_up, w_down)
 
 

time: 166 us -> 123 us (0.74)
  waiting for transfers between devices: 54.8 us -> 0 us
  Pallas kernels: 95.7 us -> 116 us
  between operations: 13.4 us -> 0.08 us
  local copies, waits for them, and re-layouts: 1.67 us -> 6.65 us
    all_gather x1 -> x0, waiting for transfers between devices: 54.8 us -> none  [on_device(): kv = lax.all_gather(own_kv, 'seq', axis=0, tiled=True)]
    pallas_call x2, Pallas kernels: 13.3 us -> 32 us  [the longest x1 25.3 us: front(): pl.pallas_call(front_kernel, in_specs=[hbm, hbm, hbm, hbm, vmem, vmem], o...]
    unnamed x1 -> x23, local copies, waits for them, and re-layouts: 1.67 us -> 6.65 us
  transfers between devices with their start and end apart: 1 -> 0, of which waited for: 1 -> 0; matrix products, arithmetic and copies ran while one was open for 0% -> 0% of each run, Pallas kernels for 0% -> 0%
where the time goes in v3:
time: 123 us
  Pallas kernels  116 us (94%)
  local copies, waits for them, and re-layouts  6.65 us (5%)
    pallas_call x1, Pallas kernels, tail(): pl.pallas_call(functools.partial(tail_kernel, lax.axis_size('head'), lax....  83.8 us
    pallas_call x1, Pallas kernels, front(): pl.pallas_call(front_kernel, in_specs=[hbm, hbm, hbm, hbm, vmem, vmem], o...  25.3 us
    pallas_call x1, Pallas kernels, attend_listed(): pl.pallas_call(attention_kernel, in_specs=[pl.BlockSpec(memory_space=pltp...  6.68 us
    unnamed x23, local copies, waits for them, and re-layouts  6.65 us

profile of v3, /device:TPU:0, one launch (start us, length us, event | category | flops | bytes accessed | tf_op | source)
XLA Modules:
  0.0 122.6 jit_solution(16052812420806197189)
XLA Ops:
  0.0 0.0 copy-start
  0.0 0.0 copy-start.1
  0.0 0.0 copy-start.2
  0.0 1.4 %copy-done.2 = bf16[2048,256]{1,0:T(8,128)(2,1)S(1)} copy-done((bf16[2048,256]{1,0:T(8,128)(2,1)S(1)}, bf16[2048,256]{1,0:T(8,128)(2,1)}, u32[]{:S(2)}) %copy-start.2) | copy-done | bytes 1048600
  1.4 0.0 copy-start.3
  1.4 2.0 %copy-done.3 = bf16[2048,256]{1,0:T(8,128)(2,1)S(1)} copy-done((bf16[2048,256]{1,0:T(8,128)(2,1)S(1)}, bf16[2048,256]{1,0:T(8,128)(2,1)}, u32[]{:S(2)}) %copy-start.3) | copy-done | bytes 1048600
  3.4 0.0 copy-start.4
  3.4 1.2 copy-done.4
  4.6 0.0 copy-start.8
  4.6 0.7 copy-done.8
  5.3 0.0 copy-start.10
  5.3 0.7 copy-done.10
  5.9 0.0 copy-start.5
  5.9 0.0 copy-start.6
  5.9 0.0 copy-start.7
  5.9 0.0 copy-start.9
  5.9 25.3 %front.1 = (bf16[8192,128]{1,0:T(8,128)(2,1)S(1)}, bf16[4,256,128]{2,1,0:T(8,128)(2,1)S(1)}, s32[4,8,128]{2,1,0:T(8,128)S(1)}) custom-call(bf16[512,2048]{1,0:T(8,128)(2,1)} %frames_hbm.3, bf16[2048,256]{1,0:T(8,128)(2,1)S(1)} %copy-done.2, bf16[2048,256]{1,0:T(8,128)(2,1)S(1)} %copy-done.3, bf16[2048,256]{1,0:T(8,128)(2,1)S(1)} %copy-done.4, ...), custom_call_target="tpu_custom_call" | custom-call | tf_op jit(solution)/shard_map/front/pallas_call | solution.py:262
  31.3 6.7 %attend.1.att_ref = bf16[4,256,128]{2,1,0:T(8,128)(2,1)S(1)} custom-call(s32[4,8,128]{2,1,0:T(8,128)S(1)} %get-tuple-element.8.tables_ref, bf16[4,256,128]{2,1,0:T(8,128)(2,1)S(1)} %get-tuple-element.9.q_ref, bf16[8192,128]{1,0:T(8,128)(2,1)S(1)} %get-tuple-element.10.kv_ref), custom_call_target="tpu_custom_call" | custom-call | tf_op jit(solution)/shard_map/attend/pallas_call | solution.py:242
  38.0 0.0 copy-done
  38.0 0.0 copy-done.1
  38.0 0.0 copy-done.5
  38.0 0.0 copy-done.6
  38.0 0.0 copy-done.7
  38.0 0.0 copy-done.9
  38.0 83.8 %tail.1 = bf16[512,256]{1,0:T(8,128)(2,1)S(1)} custom-call(bf16[4,256,128]{2,1,0:T(8,128)(2,1)S(1)} %attend.1.att_ref, bf16[256,2048]{1,0:T(8,128)(2,1)S(1)} %copy-done.5, bf16[512,2048]{1,0:T(8,128)(2,1)S(1)} %copy-done, f32[31,256]{1,0:T(8,128)S(1)} %copy-done.6, f32[1,256]{1,0:T(1,128)S(1)} %bitcast.4, f32[1,2048]{1,0:T(1,128)S(1)} %bitcast.3, ...), custom_call_target="tpu_custom_call" | custom-call | tf_op jit(solution)/shard_map/tail/pallas_call | solution.py:588
  121.9 0.7 copy.14
Async XLA Ops:
  0.0 38.0 %copy-start = (bf16[512,2048]{1,0:T(8,128)(2,1)S(1)}, bf16[512,2048]{1,0:T(8,128)(2,1)}, u32[]{:S(2)}) copy-start(bf16[512,2048]{1,0:T(8,128)(2,1)} %frames_hbm.3) | copy-start | bytes 6291460
  0.0 38.0 %copy-start.1 = (bf16[2048,1024]{1,0:T(8,128)(2,1)S(1)}, bf16[2048,1024]{1,0:T(8,128)(2,1)}, u32[]{:S(2)}) copy-start(bf16[2048,1024]{1,0:T(8,128)(2,1)} %up_hbm.1) | copy-start | bytes 12582916
  0.0 1.4 %copy-start.2 = (bf16[2048,256]{1,0:T(8,128)(2,1)S(1)}, bf16[2048,256]{1,0:T(8,128)(2,1)}, u32[]{:S(2)}) copy-start(bf16[2048,256]{1,0:T(8,128)(2,1)} %wq_hbm.1) | copy-start | bytes 3145732
  1.4 2.0 %copy-start.3 = (bf16[2048,256]{1,0:T(8,128)(2,1)S(1)}, bf16[2048,256]{1,0:T(8,128)(2,1)}, u32[]{:S(2)}) copy-start(bf16[2048,256]{1,0:T(8,128)(2,1)} %wk_hbm.1) | copy-start | bytes 3145732
  3.4 1.2 copy-start.4
  4.6 0.7 copy-start.8
  5.3 0.7 copy-start.10
  5.9 32.1 %copy-start.5 = (bf16[256,2048]{1,0:T(8,128)(2,1)S(1)}, bf16[256,2048]{1,0:T(8,128)(2,1)}, u32[]{:S(2)}) copy-start(bf16[256,2048]{1,0:T(8,128)(2,1)} %w_out_hbm.1) | copy-start | bytes 3145732
  5.9 32.1 %copy-start.6 = (f32[31,256]{1,0:T(8,128)S(1)}, f32[31,256]{1,0:T(8,128)}, u32[]{:S(2)}) copy-start(f32[31,256]{1,0:T(8,128)} %taps_ref.1) | copy-start | bytes 95236
  5.9 32.1 %copy-start.7 = (f32[2048]{0:T(1024)S(1)}, f32[2048]{0:T(1024)}, u32[]{:S(2)}) copy-start(f32[2048]{0:T(1024)} %param.19) | copy-start | bytes 24580
  5.9 32.1 %copy-start.9 = (f32[256]{0:T(256)S(1)}, f32[256]{0:T(256)}, u32[]{:S(2)}) copy-start(f32[256]{0:T(256)} %param.18) | copy-start | bytes 3076

commit v4 on v3

--- a/solution.py
+++ b/solution.py
@@ -19,6 +19,7 @@
 BLOCK = 128
 SLOTS = 8
 COUNT_ROW = 4
+LIMIT = 66_322_432
 
 
 def silu(v):
@@ -86,11 +87,13 @@
     wq_hbm,
     wk_hbm,
     wv_hbm,
+    w_out_hbm,
     lists_ref,
     counts_ref,
     kv_all,
     q_all,
     tables,
+    w_mix,
     table,
     x,
     wq,
@@ -100,6 +103,7 @@
     q_out,
     local_sems,
     sems,
+    sems_w,
 ):
     frame_rows = x.shape[0]
     half = frame_rows // 2
@@ -130,9 +134,36 @@
     mate = {"seq": seq_of(zl, y, 1 - core)}
     across = {"seq": seq_of(1 - zl, y, core)}
     barrier = pltpu.get_barrier_semaphore()
+    head = lax.axis_index("head")
+    heads = w_mix.shape[0] // w_mix.shape[1]
+
+    def head_at(d):
+        return lax.rem(head + d, heads)
+
     others = [far(d) for d in range(1, YS)] + [mate, across]
+    others += [{"head": head_at(d)} for d in range(1, heads)]
     for other in others:
         pl.semaphore_signal(barrier, inc=1, device_id=other, device_id_type=MESH)
+    pl.semaphore_wait(barrier, len(others))
+
+    width = w_mix.shape[1]
+    share = width // 2
+
+    def mix_rows(t):
+        start = pl.multiple_of(t * width + core * share, share)
+        return w_mix.at[pl.ds(start, share), :]
+
+    def w_cols(t):
+        return pl.ds(pl.multiple_of(t * width, width), width)
+
+    sent = {}
+    for d in (3, 5, 4, 1, 7, 2, 6):
+        mine = w_out_hbm.at[pl.ds(pl.multiple_of(core * share, share), share), w_cols(head_at(d))]
+        sent["w", d] = send(mine, mix_rows(head), sems_w, d, {"head": head_at(d)})
+    own_mix = pltpu.make_async_copy(
+        w_out_hbm.at[:, w_cols(head)], w_mix.at[w_cols(head), :], local_sems.at[7]
+    )
+    own_mix.start()
 
     low = lax.broadcasted_iota(jnp.int32, (half, 2 * HD), 1) < HD
     for load in loads[:3]:
@@ -146,13 +177,11 @@
             kp, vp = k[:, cols], v[:, cols]
             kv_out[2 * pair, rows, :] = jnp.where(low, kp, swap(vp)).astype(bf16)
             kv_out[2 * pair + 1, rows, :] = jnp.where(low, swap(kp), vp).astype(bf16)
-    pl.semaphore_wait(barrier, len(others))
 
     def rows_of(z_at, y_at, core_at):
         start = seq_of(z_at, y_at, core_at) * frame_rows
         return kv_all.at[pl.ds(pl.multiple_of(start, frame_rows), frame_rows), :]
 
-    sent = {}
     here = rows_of(zl, y, core)
     for d in (2, 1, 3):
         to = lax.rem(y + d, YS)
@@ -189,6 +218,10 @@
         sent["across", d].wait_recv()
         piece = rows_of(1 - zl, lax.rem(y + YS - d, YS), core)
         sent["over", d] = send(piece, piece, sems, 16 + d, mate)
+    for d in range(1, heads):
+        sent["w", d].wait_recv()
+        piece = mix_rows(head_at(heads - d))
+        sent["w_mate", d] = send(piece, piece, sems_w, heads + d, mate)
     for d in range(1, YS):
         sent["table", d].wait_recv()
     for d in range(1, YS):
@@ -197,6 +230,9 @@
         sent["mate", d].wait_recv()
     for d in range(YS):
         sent["over", d].wait_recv()
+    for d in range(1, heads):
+        sent["w_mate", d].wait_recv()
+    own_mix.wait()
     for copy in keep:
         copy.wait()
     for copy in sent.values():
@@ -244,12 +280,12 @@
         in_specs=[pl.BlockSpec(memory_space=pltpu.SMEM), vmem, vmem],
         out_specs=vmem,
         out_shape=jax.ShapeDtypeStruct(q_all.shape, jnp.bfloat16),
-        compiler_params=pltpu.CompilerParams(vmem_limit_bytes=32 * 1024 * 1024),
+        compiler_params=pltpu.CompilerParams(vmem_limit_bytes=LIMIT),
         name="attend",
     )(tables, q_all, kv_all)
 
 
-def front(frames, w_query, w_key, w_value, lists, counts):
+def front(frames, w_query, w_key, w_value, w_out, lists, counts):
     frame_rows, depth = frames.shape
     width = w_query.shape[1]
     seqs = lax.axis_size("seq")
@@ -261,12 +297,13 @@
     lanes = 2 * HD
     return pl.pallas_call(
         front_kernel,
-        in_specs=[hbm, hbm, hbm, hbm, vmem, vmem],
-        out_specs=[free, free, free],
+        in_specs=[hbm, hbm, hbm, hbm, hbm, vmem, vmem],
+        out_specs=[free, free, free, free],
         out_shape=[
             jax.ShapeDtypeStruct((seqs * frame_rows, lanes), bf16),
             jax.ShapeDtypeStruct((YS, frame_rows // 2, lanes), bf16),
             jax.ShapeDtypeStruct((YS, 8, 128), jnp.int32),
+            jax.ShapeDtypeStruct((depth, width), bf16),
         ],
         scratch_shapes=[
             pltpu.VMEM((8, 128), jnp.int32),
@@ -276,14 +313,15 @@
             pltpu.VMEM((depth, width), bf16),
             pltpu.VMEM((YS, frame_rows, lanes), bf16),
             pltpu.VMEM((YS, frame_rows // 2, lanes), bf16),
-            dma((7,)),
+            dma((8,)),
             dma((2, 24)),
+            dma((2, 16)),
         ],
         compiler_params=pltpu.CompilerParams(
-            collective_id=1, has_side_effects=True, vmem_limit_bytes=48 * 1024 * 1024
+            collective_id=1, has_side_effects=True, vmem_limit_bytes=LIMIT
         ),
         name="front",
-    )(frames, w_query, w_key, w_value, lists, counts[None, :])
+    )(frames, w_query, w_key, w_value, w_out, lists, counts[None, :])
 
 
 class Scatter:
@@ -398,7 +436,7 @@
     heads,
     seqs,
     att_ref,
-    w_out_hbm,
+    w_mix_hbm,
     frames_hbm,
     taps_ref,
     bias_ref,
@@ -406,7 +444,7 @@
     up_hbm,
     down_hbm,
     out_ref,
-    w_out,
+    w_mix,
     up,
     down,
     resid,
@@ -416,18 +454,13 @@
     second,
     whole,
     hidden,
-    relay_o,
-    direct_o,
-    sums_o,
-    z_o,
-    acc_o,
     relay_f,
     direct_f,
     sums_f,
     z_f,
     acc_f,
     ret_in,
-    attended,
+    joined,
     local_sems,
     sems_r,
     sems_o,
@@ -442,8 +475,8 @@
     get_resid = pltpu.make_async_copy(frames_hbm.at[:, own_cols], resid, local_sems.at[0])
     get_up = pltpu.make_async_copy(up_hbm, up, local_sems.at[1])
     get_down = pltpu.make_async_copy(down_hbm, down, local_sems.at[2])
-    get_out = pltpu.make_async_copy(w_out_hbm, w_out, local_sems.at[4])
-    get_out.start()
+    get_mix = pltpu.make_async_copy(w_mix_hbm, w_mix, local_sems.at[4])
+    get_mix.start()
     get_resid.start()
     get_up.start()
     get_down.start()
@@ -463,43 +496,37 @@
     for copy in back:
         copy.wait_recv()
     for pair in range(YS // 2):
-        cols = slice(pair * 2 * HD, (pair + 1) * 2 * HD)
+        cols = pl.ds(pl.multiple_of(place.me * width + pair * 2 * HD, 2 * HD), 2 * HD)
         one, two = ret_in[2 * pair].astype(jnp.float32), ret_in[2 * pair + 1].astype(jnp.float32)
-        attended[:half, cols] = jnp.where(low, one, swap(two)).astype(jnp.bfloat16)
-        attended[half:, cols] = jnp.where(low, swap(one), two).astype(jnp.bfloat16)
-
-    outer, inner = (0, PIECES - 1), tuple(range(1, PIECES - 1))
-    get_out.wait()
-    mix = Scatter(place, attended, w_out, (relay_o, direct_o, sums_o, z_o, acc_o), sems_o)
-    for p in outer:
+        joined[:half, cols] = jnp.where(low, one, swap(two)).astype(jnp.bfloat16)
+        joined[half:, cols] = jnp.where(low, swap(one), two).astype(jnp.bfloat16)
+
+    order = (0, PIECES - 1) + tuple(range(1, PIECES - 1))
+    mix = Gather(place, joined, sems_o)
+    for p in order:
         mix.first(p)
-    for p in outer:
+    for p in order:
         mix.second(p)
-    for p in inner:
-        mix.first(p)
-    for p in outer + inner:
-        mix.own(p)
-    for p in inner:
-        mix.second(p)
-    for p in outer:
+    for p in order:
         mix.third(p)
     get_resid.wait()
+    get_mix.wait()
 
     def place_stream(p):
         at = slice(p * rows, (p + 1) * rows)
-        value = (resid[at, :].astype(jnp.float32) + mix.last(p)).astype(jnp.bfloat16)
+        mix.last(p)
+        mixed = jnp.dot(joined[at, :], w_mix[...], preferred_element_type=jnp.float32)
+        value = (resid[at, :].astype(jnp.float32) + mixed).astype(jnp.bfloat16)
         stream[at, :] = value
         pad[HALO + p * rows : HALO + (p + 1) * rows, :] = value.astype(jnp.float32)
 
-    for p in outer:
+    for p in order[:2]:
         place_stream(p)
     to_before = send(stream.at[0:HALO, :], halo.at[1], sems_h, 0, place.before)
     to_after = send(
         stream.at[frame_rows - HALO : frame_rows, :], halo.at[0], sems_h, 1, place.after
     )
-    for p in inner:
-        mix.third(p)
-    for p in inner:
+    for p in order[2:]:
         place_stream(p)
     to_before.wait_recv()
     to_after.wait_recv()
@@ -509,7 +536,6 @@
     pad[HALO + frame_rows : 2 * HALO + frame_rows, :] = halo[1].astype(jnp.float32) * bottom
 
     ring = Gather(place, whole, sems_g)
-    order = (0, PIECES - 1) + tuple(range(1, PIECES - 1))
 
     def convolve(p):
         shift = HALO - KERNEL // 2
@@ -570,8 +596,8 @@
     ffn.finish()
 
 
-def tail(attended, w_out, frames, taps, bias, gain, w_up, w_down):
-    width = w_out.shape[0]
+def tail(attended, w_mix, frames, taps, bias, gain, w_up, w_down):
+    width = w_mix.shape[1]
     frame_rows, depth = frames.shape
     hidden = w_up.shape[1]
     rows = frame_rows // PIECES
@@ -591,7 +617,7 @@
         out_specs=vmem,
         out_shape=jax.ShapeDtypeStruct((frame_rows, width), bf16),
         scratch_shapes=[
-            pltpu.VMEM((width, depth), bf16),
+            pltpu.VMEM((depth, width), bf16),
             pltpu.VMEM((depth, hidden), bf16),
             pltpu.VMEM((hidden, depth), bf16),
             pltpu.VMEM((frame_rows, width), bf16),
@@ -603,22 +629,21 @@
             pltpu.VMEM((frame_rows, hidden), bf16),
         ]
         + buffers
-        + buffers
         + [
             pltpu.VMEM((YS, frame_rows // 2, 2 * HD), bf16),
-            pltpu.VMEM((frame_rows, width), bf16),
+            pltpu.VMEM((frame_rows, depth), bf16),
             dma((5,)),
             dma((2, YS)),
-            dma((2, PIECES * 4)),
+            dma((2, PIECES * 6)),
             dma((2, 2)),
             dma((2, PIECES * 6)),
             dma((2, PIECES * 4)),
         ],
         compiler_params=pltpu.CompilerParams(
-            collective_id=0, has_side_effects=True, vmem_limit_bytes=44 * 1024 * 1024
+            collective_id=0, has_side_effects=True, vmem_limit_bytes=LIMIT
         ),
         name="tail",
-    )(attended, w_out, frames, taps, bias[None, :], gain[None, :], w_up, w_down)
+    )(attended, w_mix, frames, taps, bias[None, :], gain[None, :], w_up, w_down)
 
 
 def on_device(
@@ -635,11 +660,11 @@
     block_lists,
     block_counts,
 ):
-    kv_all, q_all, tables = front(
-        frames, w_query, w_key, w_value, block_lists, block_counts
+    kv_all, q_all, tables, w_mix = front(
+        frames, w_query, w_key, w_value, w_out, block_lists, block_counts
     )
     attended = attend_listed(tables, q_all, kv_all)
-    return tail(attended, w_out, frames, conv_taps, conv_bias, norm_gain, w_up, w_down)
+    return tail(attended, w_mix, frames, conv_taps, conv_bias, norm_gain, w_up, w_down)
 
 
 def solution(mesh):

time: 123 us -> 117 us (0.951)
  local copies, waits for them, and re-layouts: 6.65 us -> 1.67 us
    pallas_call x1, Pallas kernels: 83.8 us -> 75.3 us  [tail(): pl.pallas_call(functools.partial(tail_kernel, lax.axis_size('head'), lax....]
    pallas_call x1, Pallas kernels: 25.3 us -> 31.4 us  [front(): pl.pallas_call(front_kernel, in_specs=[hbm, hbm, hbm, hbm, hbm, vmem, vme...]
    unnamed x23 -> x1, local copies, waits for them, and re-layouts: 6.65 us -> 1.67 us
    pallas_call x1, Pallas kernels: 6.68 us -> 8.3 us  [attend_listed(): pl.pallas_call(attention_kernel, in_specs=[pl.BlockSpec(memory_space=pltp...]
where the time goes in v4:
time: 117 us
  Pallas kernels  115 us (98%)
  local copies, waits for them, and re-layouts  1.67 us (1%)
    pallas_call x1, Pallas kernels, tail(): pl.pallas_call(functools.partial(tail_kernel, lax.axis_size('head'), lax....  75.3 us
    pallas_call x1, Pallas kernels, front(): pl.pallas_call(front_kernel, in_specs=[hbm, hbm, hbm, hbm, hbm, vmem, vme...  31.4 us
    pallas_call x1, Pallas kernels, attend_listed(): pl.pallas_call(attention_kernel, in_specs=[pl.BlockSpec(memory_space=pltp...  8.3 us

profile of v4, /device:TPU:0, one launch (start us, length us, event | category | flops | bytes accessed | tf_op | source)
XLA Modules:
  0.0 116.7 jit_solution(10394119640974544115)
XLA Ops:
  0.0 31.4 %front.1 = (bf16[8192,128]{1,0:T(8,128)(2,1)}, bf16[4,256,128]{2,1,0:T(8,128)(2,1)}, s32[4,8,128]{2,1,0:T(8,128)}, bf16[2048,256]{1,0:T(8,128)(2,1)}) custom-call(bf16[512,2048]{1,0:T(8,128)(2,1)} %frames_hbm.3, bf16[2048,256]{1,0:T(8,128)(2,1)} %wq_hbm.1, bf16[2048,256]{1,0:T(8,128)(2,1)} %wk_hbm.1, bf16[2048,256]{1,0:T(8,128)(2,1)} %wv_hbm.1, ...), custom_call_target="tpu_custom_call" | custom-call | tf_op jit(solution)/shard_map/front/pallas_call | solution.py:298
  31.4 8.3 %attend.1.att_ref = bf16[4,256,128]{2,1,0:T(8,128)(2,1)} custom-call(s32[4,8,128]{2,1,0:T(8,128)} %get-tuple-element.9.tables_ref, bf16[4,256,128]{2,1,0:T(8,128)(2,1)} %get-tuple-element.10.q_ref, bf16[8192,128]{1,0:T(8,128)(2,1)} %get-tuple-element.11.kv_ref), custom_call_target="tpu_custom_call" | custom-call | tf_op jit(solution)/shard_map/attend/pallas_call | solution.py:278
  39.7 75.3 %tail.1 = bf16[512,256]{1,0:T(8,128)(2,1)} custom-call(bf16[4,256,128]{2,1,0:T(8,128)(2,1)} %attend.1.att_ref, bf16[2048,256]{1,0:T(8,128)(2,1)} %get-tuple-element.12.w_mix_hbm, bf16[512,2048]{1,0:T(8,128)(2,1)} %frames_hbm.3, f32[31,256]{1,0:T(8,128)} %taps_ref.1, f32[1,256]{1,0:T(1,128)} %bitcast.4, f32[1,2048]{1,0:T(1,128)} %bitcast.3, ...), custom_call_target="tpu_custom_call" | custom-call | tf_op jit(solution)/shard_map/tail/pallas_call | solution.py:614
  115.0 1.7 %copy.14 = bf16[512,256]{1,0:T(8,128)(2,1)} copy(bf16[512,256]{1,0:T(8,128)(2,1)} %tail.1) | data formatting | bytes 524288

commit v5 on v4

--- a/solution.py
+++ b/solution.py
@@ -14,12 +14,16 @@
 
 MESH = pl.DeviceIdType.MESH
 PIECES = 4
+LAG = PIECES // 4
+ORDER = (0, 2, 1, 3)
+INSIDE, EDGES = (1, 2), (0, 3)
 HALO = 16
 YS = 4
 BLOCK = 128
 SLOTS = 8
 COUNT_ROW = 4
-LIMIT = 66_322_432
+FRONT_LIMIT = 66322432
+LIMIT = 66322432
 
 
 def silu(v):
@@ -318,7 +322,7 @@
             dma((2, 16)),
         ],
         compiler_params=pltpu.CompilerParams(
-            collective_id=1, has_side_effects=True, vmem_limit_bytes=LIMIT
+            collective_id=1, has_side_effects=True, vmem_limit_bytes=FRONT_LIMIT
         ),
         name="front",
     )(frames, w_query, w_key, w_value, w_out, lists, counts[None, :])
@@ -482,29 +486,41 @@
     get_down.start()
     place.greet()
 
-    back = [
-        send(att_ref.at[lax.rem(place.y + d, YS)], ret_in.at[place.y], sems_r, d, place.far(d))
-        for d in (2, 1, 3)
-    ]
+    share = att_ref.shape[1] // 2
+    back = {}
+    for h in (0, 1):
+        at = slice(h * share, (h + 1) * share)
+        for d in (1, 3, 2):
+            back[d, h] = send(
+                att_ref.at[lax.rem(place.y + d, YS), at, :],
+                ret_in.at[place.y, at, :],
+                sems_r,
+                h * YS + d,
+                place.far(d),
+            )
     own_back = pltpu.make_async_copy(
         att_ref.at[place.y], ret_in.at[place.y], local_sems.at[3]
     )
     own_back.start()
     half = frame_rows // 2
-    low = lax.broadcasted_iota(jnp.int32, (half, 2 * HD), 1) < HD
+    low = lax.broadcasted_iota(jnp.int32, (share, 2 * HD), 1) < HD
+    mix = Gather(place, joined, sems_o)
+    order = ORDER
+    ahead_rows = {0: (0, 2), 1: (1, 3)}
     own_back.wait()
-    for copy in back:
-        copy.wait_recv()
-    for pair in range(YS // 2):
-        cols = pl.ds(pl.multiple_of(place.me * width + pair * 2 * HD, 2 * HD), 2 * HD)
-        one, two = ret_in[2 * pair].astype(jnp.float32), ret_in[2 * pair + 1].astype(jnp.float32)
-        joined[:half, cols] = jnp.where(low, one, swap(two)).astype(jnp.bfloat16)
-        joined[half:, cols] = jnp.where(low, swap(one), two).astype(jnp.bfloat16)
-
-    order = (0, PIECES - 1) + tuple(range(1, PIECES - 1))
-    mix = Gather(place, joined, sems_o)
-    for p in order:
-        mix.first(p)
+    for h in (0, 1):
+        for d in (1, 3, 2):
+            back[d, h].wait_recv()
+        at = slice(h * share, (h + 1) * share)
+        later = slice(half + h * share, half + (h + 1) * share)
+        for pair in range(YS // 2):
+            cols = pl.ds(pl.multiple_of(place.me * width + pair * 2 * HD, 2 * HD), 2 * HD)
+            one = ret_in[2 * pair, at, :].astype(jnp.float32)
+            two = ret_in[2 * pair + 1, at, :].astype(jnp.float32)
+            joined[at, cols] = jnp.where(low, one, swap(two)).astype(jnp.bfloat16)
+            joined[later, cols] = jnp.where(low, swap(one), two).astype(jnp.bfloat16)
+        for p in ahead_rows[h]:
+            mix.first(p)
     for p in order:
         mix.second(p)
     for p in order:
@@ -520,21 +536,14 @@
         stream[at, :] = value
         pad[HALO + p * rows : HALO + (p + 1) * rows, :] = value.astype(jnp.float32)
 
-    for p in order[:2]:
+    for p in order:
         place_stream(p)
-    to_before = send(stream.at[0:HALO, :], halo.at[1], sems_h, 0, place.before)
-    to_after = send(
-        stream.at[frame_rows - HALO : frame_rows, :], halo.at[0], sems_h, 1, place.after
-    )
-    for p in order[2:]:
-        place_stream(p)
-    to_before.wait_recv()
-    to_after.wait_recv()
-    top = jnp.where(place.s == 0, 0.0, 1.0)
-    bottom = jnp.where(place.s == seqs - 1, 0.0, 1.0)
-    pad[0:HALO, :] = halo[0].astype(jnp.float32) * top
-    pad[HALO + frame_rows : 2 * HALO + frame_rows, :] = halo[1].astype(jnp.float32) * bottom
-
+        if p == 0:
+            to_before = send(stream.at[0:HALO, :], halo.at[1], sems_h, 0, place.before)
+        if p == PIECES - 1:
+            to_after = send(
+                stream.at[frame_rows - HALO : frame_rows, :], halo.at[0], sems_h, 1, place.after
+            )
     ring = Gather(place, whole, sems_g)
 
     def convolve(p):
@@ -560,34 +569,47 @@
         upper = jnp.dot(normed, up[...], preferred_element_type=jnp.float32)
         hidden[at, :] = silu(upper).astype(jnp.bfloat16)
 
-    for p in order:
+    order = INSIDE + EDGES
+    for p in INSIDE:
+        convolve(p)
+        ring.first(p)
+    to_before.wait_recv()
+    to_after.wait_recv()
+    top = jnp.where(place.s == 0, 0.0, 1.0)
+    bottom = jnp.where(place.s == seqs - 1, 0.0, 1.0)
+    pad[0:HALO, :] = halo[0].astype(jnp.float32) * top
+    pad[HALO + frame_rows : 2 * HALO + frame_rows, :] = halo[1].astype(jnp.float32) * bottom
+
+    for p in EDGES:
         convolve(p)
         ring.first(p)
     for p in order:
         ring.second(p)
-    for p in order[:2]:
+    ahead = 2 * LAG
+    for p in order[:ahead]:
         ring.third(p)
     get_up.wait()
     get_down.wait()
     ffn = Scatter(place, hidden, down, (relay_f, direct_f, sums_f, z_f, acc_f), sems_f)
     for i, p in enumerate(order):
-        if i + 2 < PIECES:
-            ring.third(order[i + 2])
+        if i + ahead < PIECES:
+            ring.third(order[i + ahead])
         ring.last(p)
         feed(p)
         ffn.first(p)
-        if i >= 1:
-            ffn.second(order[i - 1])
+        if i >= LAG:
+            ffn.second(order[i - LAG])
         ffn.own(p)
-        if i >= 2:
-            ffn.third(order[i - 2])
-    ffn.second(order[-1])
-    for p in order[-2:]:
+        if i >= 2 * LAG:
+            ffn.third(order[i - 2 * LAG])
+    for p in order[PIECES - LAG :]:
+        ffn.second(p)
+    for p in order[PIECES - 2 * LAG :]:
         ffn.third(p)
     for p in order:
         at = slice(p * rows, (p + 1) * rows)
         out_ref[at, :] = (second[at, :].astype(jnp.float32) + ffn.last(p)).astype(out_ref.dtype)
-    for copy in back:
+    for copy in back.values():
         copy.wait_send()
     mix.finish()
     to_before.wait_send()
@@ -633,7 +655,7 @@
             pltpu.VMEM((YS, frame_rows // 2, 2 * HD), bf16),
             pltpu.VMEM((frame_rows, depth), bf16),
             dma((5,)),
-            dma((2, YS)),
+            dma((2, 2 * YS)),
             dma((2, PIECES * 6)),
             dma((2, 2)),
             dma((2, PIECES * 6)),

time: 117 us -> 115 us (0.983); the launches traced: 117 us -> 113 us
  Pallas kernels: 115 us -> 111 us
    pallas_call x1, Pallas kernels: 75.3 us -> 71.7 us  [tail(): pl.pallas_call(functools.partial(tail_kernel, lax.axis_size('head'), lax....]
where the time goes in v5:
time: 115 us; the launch traced here: 113 us
  Pallas kernels  111 us (97%)
  local copies, waits for them, and re-layouts  1.67 us (1%)
    pallas_call x1, Pallas kernels, tail(): pl.pallas_call(functools.partial(tail_kernel, lax.axis_size('head'), lax....  71.7 us
    pallas_call x1, Pallas kernels, front(): pl.pallas_call(front_kernel, in_specs=[hbm, hbm, hbm, hbm, hbm, vmem, vme...  31.4 us
    pallas_call x1, Pallas kernels, attend_listed(): pl.pallas_call(attention_kernel, in_specs=[pl.BlockSpec(memory_space=pltp...  8.3 us

profile of v5, /device:TPU:0, one launch (start us, length us, event | category | flops | bytes accessed | tf_op | source)
XLA Modules:
  0.0 113.1 jit_solution(4669541449343830934)
XLA Ops:
  0.0 31.4 %front.1 = (bf16[8192,128]{1,0:T(8,128)(2,1)}, bf16[4,256,128]{2,1,0:T(8,128)(2,1)}, s32[4,8,128]{2,1,0:T(8,128)}, bf16[2048,256]{1,0:T(8,128)(2,1)}) custom-call(bf16[512,2048]{1,0:T(8,128)(2,1)} %frames_hbm.3, bf16[2048,256]{1,0:T(8,128)(2,1)} %wq_hbm.1, bf16[2048,256]{1,0:T(8,128)(2,1)} %wk_hbm.1, bf16[2048,256]{1,0:T(8,128)(2,1)} %wv_hbm.1, ...), custom_call_target="tpu_custom_call" | custom-call | tf_op jit(solution)/shard_map/front/pallas_call | solution.py:302
  31.4 8.3 %attend.1.att_ref = bf16[4,256,128]{2,1,0:T(8,128)(2,1)} custom-call(s32[4,8,128]{2,1,0:T(8,128)} %get-tuple-element.9.tables_ref, bf16[4,256,128]{2,1,0:T(8,128)(2,1)} %get-tuple-element.10.q_ref, bf16[8192,128]{1,0:T(8,128)(2,1)} %get-tuple-element.11.kv_ref), custom_call_target="tpu_custom_call" | custom-call | tf_op jit(solution)/shard_map/attend/pallas_call | solution.py:282
  39.7 71.7 %tail.1 = bf16[512,256]{1,0:T(8,128)(2,1)} custom-call(bf16[4,256,128]{2,1,0:T(8,128)(2,1)} %attend.1.att_ref, bf16[2048,256]{1,0:T(8,128)(2,1)} %get-tuple-element.12.w_mix_hbm, bf16[512,2048]{1,0:T(8,128)(2,1)} %frames_hbm.3, f32[31,256]{1,0:T(8,128)} %taps_ref.1, f32[1,256]{1,0:T(1,128)} %bitcast.4, f32[1,2048]{1,0:T(1,128)} %bitcast.3, ...), custom_call_target="tpu_custom_call" | custom-call | tf_op jit(solution)/shard_map/tail/pallas_call | solution.py:636
  111.5 1.7 %copy.14 = bf16[512,256]{1,0:T(8,128)(2,1)} copy(bf16[512,256]{1,0:T(8,128)(2,1)} %tail.1) | data formatting | bytes 524288

commit v6 on v5

--- a/solution.py
+++ b/solution.py
@@ -148,8 +148,6 @@
     others += [{"head": head_at(d)} for d in range(1, heads)]
     for other in others:
         pl.semaphore_signal(barrier, inc=1, device_id=other, device_id_type=MESH)
-    pl.semaphore_wait(barrier, len(others))
-
     width = w_mix.shape[1]
     share = width // 2
 
@@ -159,15 +157,6 @@
 
     def w_cols(t):
         return pl.ds(pl.multiple_of(t * width, width), width)
-
-    sent = {}
-    for d in (3, 5, 4, 1, 7, 2, 6):
-        mine = w_out_hbm.at[pl.ds(pl.multiple_of(core * share, share), share), w_cols(head_at(d))]
-        sent["w", d] = send(mine, mix_rows(head), sems_w, d, {"head": head_at(d)})
-    own_mix = pltpu.make_async_copy(
-        w_out_hbm.at[:, w_cols(head)], w_mix.at[w_cols(head), :], local_sems.at[7]
-    )
-    own_mix.start()
 
     low = lax.broadcasted_iota(jnp.int32, (half, 2 * HD), 1) < HD
     for load in loads[:3]:
@@ -186,13 +175,23 @@
         start = seq_of(z_at, y_at, core_at) * frame_rows
         return kv_all.at[pl.ds(pl.multiple_of(start, frame_rows), frame_rows), :]
 
+    pl.semaphore_wait(barrier, len(others))
+    sent = {}
     here = rows_of(zl, y, core)
-    for d in (2, 1, 3):
+    sent["across", 0] = send(kv_out.at[y], here, sems, 8, across)
+    for d in (1, 3, 2):
         to = lax.rem(y + d, YS)
         sent["kv", d] = send(kv_out.at[to], here, sems, d, far(d))
         sent["table", d] = send(table, tables.at[y], sems, 4 + d, far(d))
-    sent["across", 0] = send(kv_out.at[y], here, sems, 8, across)
     sent["mate", 0] = send(kv_out.at[y], here, sems, 12, mate)
+    for d in (3, 5, 4, 1, 7, 2, 6):
+        mine = w_out_hbm.at[pl.ds(pl.multiple_of(core * share, share), share), w_cols(head_at(d))]
+        sent["w", d] = send(mine, mix_rows(head), sems_w, d, {"head": head_at(d)})
+    own_mix = pltpu.make_async_copy(
+        w_out_hbm.at[:, w_cols(head)], w_mix.at[w_cols(head), :], local_sems.at[7]
+    )
+    own_mix.start()
+
     keep = [
         pltpu.make_async_copy(kv_out.at[y], here, local_sems.at[4]),
         pltpu.make_async_copy(table, tables.at[y], local_sems.at[5]),
@@ -600,11 +599,11 @@
         if i >= LAG:
             ffn.second(order[i - LAG])
         ffn.own(p)
-        if i >= 2 * LAG:
+        if 2 * LAG <= i < PIECES - LAG:
             ffn.third(order[i - 2 * LAG])
     for p in order[PIECES - LAG :]:
         ffn.second(p)
-    for p in order[PIECES - 2 * LAG :]:
+    for p in order[PIECES - 3 * LAG :]:
         ffn.third(p)
     for p in order:
         at = slice(p * rows, (p + 1) * rows)

time: 115 us -> 114 us (level)
    pallas_call x1, Pallas kernels: 31.4 us -> 28.2 us  [front(): pl.pallas_call(front_kernel, in_specs=[hbm, hbm, hbm, hbm, hbm, vmem, vme...]
    pallas_call x1, Pallas kernels: 71.7 us -> 74.6 us  [tail(): pl.pallas_call(functools.partial(tail_kernel, lax.axis_size('head'), lax....]
where the time goes in v6:
time: 114 us; the launch traced here: 113 us
  Pallas kernels  111 us (97%)
  local copies, waits for them, and re-layouts  1.67 us (1%)
    pallas_call x1, Pallas kernels, tail(): pl.pallas_call(functools.partial(tail_kernel, lax.axis_size('head'), lax....  74.6 us
    pallas_call x1, Pallas kernels, front(): pl.pallas_call(front_kernel, in_specs=[hbm, hbm, hbm, hbm, hbm, vmem, vme...  28.2 us
    pallas_call x1, Pallas kernels, attend_listed(): pl.pallas_call(attention_kernel, in_specs=[pl.BlockSpec(memory_space=pltp...  8.3 us

profile of v6, /device:TPU:0, one launch (start us, length us, event | category | flops | bytes accessed | tf_op | source)
XLA Modules:
  0.0 112.9 jit_solution(17815032068765052574)
XLA Ops:
  0.0 28.2 %front.1 = (bf16[8192,128]{1,0:T(8,128)(2,1)}, bf16[4,256,128]{2,1,0:T(8,128)(2,1)}, s32[4,8,128]{2,1,0:T(8,128)}, bf16[2048,256]{1,0:T(8,128)(2,1)}) custom-call(bf16[512,2048]{1,0:T(8,128)(2,1)} %frames_hbm.3, bf16[2048,256]{1,0:T(8,128)(2,1)} %wq_hbm.1, bf16[2048,256]{1,0:T(8,128)(2,1)} %wk_hbm.1, bf16[2048,256]{1,0:T(8,128)(2,1)} %wv_hbm.1, ...), custom_call_target="tpu_custom_call" | custom-call | tf_op jit(solution)/shard_map/front/pallas_call | solution.py:301
  28.3 8.3 %attend.1.att_ref = bf16[4,256,128]{2,1,0:T(8,128)(2,1)} custom-call(s32[4,8,128]{2,1,0:T(8,128)} %get-tuple-element.9.tables_ref, bf16[4,256,128]{2,1,0:T(8,128)(2,1)} %get-tuple-element.10.q_ref, bf16[8192,128]{1,0:T(8,128)(2,1)} %get-tuple-element.11.kv_ref), custom_call_target="tpu_custom_call" | custom-call | tf_op jit(solution)/shard_map/attend/pallas_call | solution.py:281
  36.6 74.6 %tail.1 = bf16[512,256]{1,0:T(8,128)(2,1)} custom-call(bf16[4,256,128]{2,1,0:T(8,128)(2,1)} %attend.1.att_ref, bf16[2048,256]{1,0:T(8,128)(2,1)} %get-tuple-element.12.w_mix_hbm, bf16[512,2048]{1,0:T(8,128)(2,1)} %frames_hbm.3, f32[31,256]{1,0:T(8,128)} %taps_ref.1, f32[1,256]{1,0:T(1,128)} %bitcast.4, f32[1,2048]{1,0:T(1,128)} %bitcast.3, ...), custom_call_target="tpu_custom_call" | custom-call | tf_op jit(solution)/shard_map/tail/pallas_call | solution.py:635
  111.2 1.7 %copy.14 = bf16[512,256]{1,0:T(8,128)(2,1)} copy(bf16[512,256]{1,0:T(8,128)(2,1)} %tail.1) | data formatting | bytes 524288
